TPU v7x, 32 devices: a whole 2x2x4 slice. The times are simulated.
32 devices in a mesh: tgt: 8 (over z, core), sup: 4 (over y, x).
Axes of the slice: x: 2, y: 2, z: 4, core: 2. Of those that a mesh axis runs over, the one named last changes fastest.
Arguments:
- target_pool: float32 [512, 3, 1024], P('tgt'), may hold values from -6 to 6
- target_index: int32 [64], P('tgt'), may hold values from 0 to 511, as said below
- target_labels: int32 [64], P('tgt'), may hold values from 0 to 99
- dual_weights: float32 [128, 100], P('sup'), may hold values from -0.5 to 0.5
- support_images: float32 [128, 3, 1024], P(('sup', 'tgt')), may hold values from -6 to 6
Outputs:
- residual: float32 [64, 100], P('tgt')
- support_grad: float32 [128, 3, 1024], P(('sup', 'tgt'))
Inputs may be any that keep to these rules, and one draw needn't show every extreme that they name: `target_index`: for each j, the targets 8 * j to 8 * (j + 1) - 1 name distinct candidates among 64 * j to 64 * (j + 1) - 1.
All inputs are finite; a program needn't handle non-finite values.
Results may differ from a plain program's by a relative error of at most 0.0003.
Values sent between devices are 32-bit elements; how exact they have to be, the bound alone decides.
A program may use at most 64 MiB of HBM per device.

v0:
```python
import functools
import math

import jax
import jax.numpy as jnp
from jax import lax
from jax.experimental import pallas as pl
from jax.experimental.pallas import tpu as pltpu
from jax.sharding import PartitionSpec as P

CHANNELS = 3
SIDE = 32
CLASSES = 100
LAYERS = 3
PIXELS = 1024
BETA = 0.01
PACK = 4
SUB = 8
LANES = 128
MESH = pl.DeviceIdType.MESH
HIGH = lax.Precision.HIGHEST
ACOS = (
    1.5707963050,
    -0.2145988016,
    0.0889789874,
    -0.0501743046,
    0.0308918810,
    -0.0170881256,
    0.0066700901,
    -0.0012624911,
)


def masks():
    lane = lax.broadcasted_iota(jnp.int32, (SUB, LANES), 1)
    row = lax.broadcasted_iota(jnp.int32, (SUB, LANES), 0)
    column = lane % SIDE
    return (column > 0, column < SIDE - 1, row > 0, row < SUB - 1, lane // SIDE)


def box_sum(maps, mask):
    right, left, down, up, _ = mask
    axis = maps[0].ndim - 1

    def across(v):
        return (
            v
            + jnp.where(right, pltpu.roll(v, 1, axis), 0.0)
            + jnp.where(left, pltpu.roll(v, LANES - 1, axis), 0.0)
        )

    before = jnp.where(down, pltpu.roll(maps[3], 1, axis - 1), 0.0)
    after = jnp.where(up, pltpu.roll(maps[0], SUB - 1, axis - 1), 0.0)
    low = maps[0] + maps[1]
    high = maps[2] + maps[3]
    return [across(v) for v in (before + low, low + maps[2], maps[1] + high, high + after)]


def interleave(images, mask):
    group = mask[4]
    out = []
    for k in range(PACK):
        total = None
        for m in range(PACK):
            shift = ((m - k) * SIDE) % LANES
            moved = images[m] if shift == 0 else pltpu.roll(images[m], shift, 1)
            total = moved if total is None else jnp.where(group == m, moved, total)
        out.append(total)
    return out


def replicate(image, mask):
    group = mask[4]
    out = []
    rolled = [image] + [pltpu.roll(image, SIDE * s, 1) for s in range(1, PACK)]
    for k in range(PACK):
        total = None
        for m in range(PACK):
            moved = rolled[(m - k) % PACK]
            total = moved if total is None else jnp.where(group == m, moved, total)
        out.append(total)
    return out


def levels_of(images, mask):
    energy = []
    for k in range(PACK):
        total = images[0][k] * images[0][k]
        for channel in range(1, CHANNELS):
            total = total + images[channel][k] * images[channel][k]
        energy.append(total * (1.0 / CHANNELS))
    levels = []
    current = energy
    for _ in range(LAYERS):
        current = [v * (1.0 / 9.0) + BETA for v in box_sum(current, mask)]
        levels.append(current)
    return levels


def kernel(
    nt, ns, own_t, own_s,
    index_ref, label_ref, pool_ref, dual_ref, support_ref,
    residual_ref, grad_ref,
    tbuf, dbuf, kbuf, srep, sroot, tlev, amp, ang, ksum, wexp, accl, accc, pred, flat,
    plane_send, plane_recv, part_send, part_recv, dual_send, dual_recv, k_send, k_recv, ready,
):
    ti = lax.axis_index("tgt")
    si = lax.axis_index("sup")
    chips = nt // 2
    chip = ti // 2
    core = ti % 2
    ndev = nt * ns
    me = si * nt + ti
    groups_own = own_t // PACK
    groups = nt * groups_own
    images = groups_own * CHANNELS * PACK
    targets = nt * own_t
    mask = masks()

    barrier = pltpu.get_barrier_semaphore()

    def others(action):
        for s in range(ns):
            for t in range(nt):
                pl.when((si != s) | (ti != t))(functools.partial(action, t, s))

    def greet(t, s):
        pl.semaphore_signal(barrier, inc=1, device_id=(t, s), device_id_type=MESH)

    for s in range(ns):
        pl.when(si != s)(functools.partial(greet, ti, s))
    for t in range(nt):
        pl.when(ti != t)(functools.partial(greet, t, si))

    pool = pool_ref.shape[1] * SUB
    picks = [lax.rem(index_ref[t], pool) for t in range(own_t)]
    for gl in range(groups_own):
        for channel in range(CHANNELS):
            natural = [
                pool_ref[channel, at // SUB, :, pl.ds(at % SUB, 1), :].reshape(SUB, LANES)
                for at in picks[gl * PACK : (gl + 1) * PACK]
            ]
            phases = interleave(natural, mask)
            for k in range(PACK):
                tbuf[ti, (gl * CHANNELS + channel) * PACK + k] = phases[k]
    row = lax.broadcasted_iota(jnp.int32, (SUB, LANES), 0)
    lane = lax.broadcasted_iota(jnp.int32, (SUB, LANES), 1)
    label = jnp.zeros((SUB, LANES), jnp.int32)
    for r in range(own_t):
        label = jnp.where(row == r, label_ref[r], label)
    own_onehot = jnp.where(label == lane, 1.0, 0.0).astype(jnp.float32)
    tbuf[ti, images] = own_onehot
    dbuf[si] = dual_ref[...]

    pl.semaphore_wait(barrier, nt + ns - 2)

    def chunk(owner, gl):
        first = gl * CHANNELS * PACK
        last = images + 1 if gl == groups_own - 1 else first + CHANNELS * PACK
        return tbuf.at[owner, pl.ds(first, last - first)]

    def plane_copy(source_chip, gl, way, target_chip):
        part = chunk(source_chip * 2 + core, gl)
        return pltpu.make_async_remote_copy(
            src_ref=part,
            dst_ref=part,
            send_sem=plane_send.at[way, source_chip, gl],
            recv_sem=plane_recv.at[source_chip, gl],
            device_id=(target_chip * 2 + core, si),
            device_id_type=MESH,
        )

    def part_copy(p, gl, side):
        part = chunk(p * 2 + side, gl)
        return pltpu.make_async_remote_copy(
            src_ref=part,
            dst_ref=part,
            send_sem=part_send.at[p, gl],
            recv_sem=part_recv.at[p, gl],
            device_id=(chip * 2 + 1 - core, si),
            device_id_type=MESH,
        )

    def handle(h, gl):
        for way in range(2):
            step = 1 - 2 * way
            source = chip - step * h
            onward = chip + step

            @pl.when((source >= 0) & (source < chips))
            def _():
                plane_copy(source, gl, way, source).wait_recv()

                @pl.when((onward >= 0) & (onward < chips))
                def _():
                    plane_copy(source, gl, way, onward).start()

                part_copy(source, gl, core).start()

    def dual_copy(s):
        return pltpu.make_async_remote_copy(
            src_ref=dbuf.at[si],
            dst_ref=dbuf.at[si],
            send_sem=dual_send.at[s],
            recv_sem=dual_recv.at[si],
            device_id=(ti, s),
            device_id_type=MESH,
        )

    def dual_arrival(s):
        return pltpu.make_async_remote_copy(
            src_ref=dbuf.at[s],
            dst_ref=dbuf.at[s],
            send_sem=dual_send.at[s],
            recv_sem=dual_recv.at[s],
            device_id=(ti, s),
            device_id_type=MESH,
        )

    def k_copy(t, s):
        return pltpu.make_async_remote_copy(
            src_ref=kbuf.at[me],
            dst_ref=kbuf.at[me],
            send_sem=k_send,
            recv_sem=k_recv,
            device_id=(t, s),
            device_id_type=MESH,
        )

    def k_all():
        others_slots = kbuf.at[pl.ds(0, ndev - 1)]
        return pltpu.make_async_remote_copy(
            src_ref=others_slots,
            dst_ref=others_slots,
            send_sem=k_send,
            recv_sem=k_recv,
            device_id=(1 - core + chip * 2, si),
            device_id_type=MESH,
        )

    for gl in range(groups_own):
        for way in range(2):
            onward = chip + 1 - 2 * way

            @pl.when((onward >= 0) & (onward < chips))
            def _():
                plane_copy(chip, gl, way, onward).start()

        part_copy(chip, gl, core).start()

    def vouch(t):
        pl.semaphore_signal(ready, inc=1, device_id=(t, si), device_id_type=MESH)

    for t in range(nt):
        pl.when(ti != t)(functools.partial(vouch, t))

    def send_dual(step, carry):
        dual_copy(lax.rem(si + step, ns)).start()
        return carry

    lax.fori_loop(1, ns, send_dual, 0)

    for m in range(own_s):
        reps = []
        for channel in range(CHANNELS):
            phases = replicate(support_ref[channel, :, m, :], mask)
            reps.append(phases)
            for k in range(PACK):
                srep[channel, k, m] = phases[k]
        levels = levels_of(reps, mask)
        for layer in range(LAYERS):
            for k in range(PACK):
                inverse = lax.rsqrt(levels[layer][k])
                sroot[layer, 0, k, m] = inverse * (1.0 / 9.0**layer)
                sroot[layer, 1, k, m] = levels[layer][k] * inverse * (9.0**layer / math.pi)

    def group_forward(owner, gl):
        g = owner * groups_own + gl
        image = [
            [tbuf[owner, (gl * CHANNELS + channel) * PACK + k] for k in range(PACK)]
            for channel in range(CHANNELS)
        ]
        levels = levels_of(image, mask)
        for layer in range(LAYERS):
            for k in range(PACK):
                inverse = lax.rsqrt(levels[layer][k])
                tlev[layer, 0, k] = inverse
                tlev[layer, 1, k] = levels[layer][k] * inverse
        current = []
        for k in range(PACK):
            total = image[0][k][None] * srep[0, k]
            for channel in range(1, CHANNELS):
                total = total + image[channel][k][None] * srep[channel, k]
            current.append(total)
        cross = [v * (1.0 / 27.0) + BETA for v in box_sum(current, mask)]
        for layer in range(LAYERS):
            mapped = []
            for k in range(PACK):
                x = cross[k] * (tlev[layer, 0, k][None] * sroot[layer, 0, k])
                size = jnp.abs(x)
                gap = jnp.maximum(1.0 - size, 1e-20)
                rest = 1.0 + size
                half = gap * lax.rsqrt(gap)
                poly = size * (ACOS[7] / math.pi) + ACOS[6] / math.pi
                for term in ACOS[5::-1]:
                    poly = poly * size + term / math.pi
                near = half * poly
                slope = jnp.where(x >= 0.0, 1.0 - near, near)
                sine = half * (rest * lax.rsqrt(rest))
                scaled = sine * tlev[layer, 1, k][None]
                amp[g, layer, k] = scaled
                ang[g, layer, k] = slope
                mapped.append(scaled * sroot[layer, 1, k] + slope * cross[k])
            if layer + 1 < LAYERS:
                cross = [v + BETA * 9.0 ** (layer + 1) for v in box_sum(mapped, mask)]
        total = (mapped[0] + mapped[1]) + (mapped[2] + mapped[3])
        ksum[:, pl.ds(g, 1), :] = jnp.sum(total, axis=1, keepdims=True)

    def order(n):
        both = jnp.minimum(chip, chips - 1 - chip)
        h = (n + 1) // 2
        two_sided = jnp.where(n % 2 == 1, chip - h, chip + h)
        far = n - both
        one_sided = jnp.where(chip <= chips - 1 - chip, chip + far, chip - far)
        return jnp.where(n <= 2 * both, two_sided, one_sided)

    def visit(slot, carry):
        n = slot // (2 * groups_own)
        at = slot % (2 * groups_own)
        gl = at % groups_own
        p = order(n)
        for later in range(1, groups_own):
            pl.when((n > 0) & (at == later))(functools.partial(handle, n, later))
        pl.when((n + 1 < chips) & (at == 2 * groups_own - 1))(functools.partial(handle, n + 1, 0))
        for which in range(groups_own):
            @pl.when(at == groups_own + which)
            def _():
                part_copy(p, which, 1 - core).wait_recv()

        side = jnp.where(at < groups_own, core, 1 - core)
        group_forward(p * 2 + side, gl)
        return carry

    lax.fori_loop(0, 2 * groups_own * chips, visit, 0)

    spread_row = lax.broadcasted_iota(jnp.int32, (targets, LANES), 0)
    spread_lane = lax.broadcasted_iota(jnp.int32, (targets, LANES), 1)
    spread = jnp.where(spread_row % PACK == spread_lane // SIDE, 1.0, 0.0).astype(jnp.float32)
    keep_g = lax.broadcasted_iota(jnp.int32, (groups, targets), 0)
    keep_t = lax.broadcasted_iota(jnp.int32, (groups, targets), 1)
    keep = jnp.where(keep_t // PACK == keep_g, 1.0, 0.0).astype(jnp.float32)
    nt_dims = (((1,), (1,)), ((), ()))
    lane_sums = lax.dot_general(
        ksum[...].reshape(own_s * groups, LANES), spread, nt_dims,
        precision=HIGH, preferred_element_type=jnp.float32,
    ) * (1.0 / (PIXELS * 9.0 ** (LAYERS - 1)))
    picked = jnp.sum(lane_sums.reshape(own_s, groups, targets) * keep[None], axis=1)
    kbuf[me] = picked

    pl.semaphore_wait(ready, nt - 1)
    others(lambda t, s: k_copy(t, s).start())

    def take_dual(step, carry):
        dual_arrival(lax.rem(si + step, ns)).wait_recv()
        return carry

    lax.fori_loop(1, ns, take_dual, 0)
    duals = dbuf[...].reshape(ns * dual_ref.shape[0], CLASSES)
    own_duals = dual_ref[pl.ds(ti * own_s, own_s), :]
    gram = lax.dot_general(
        own_duals, duals, nt_dims, precision=HIGH, preferred_element_type=jnp.float32
    )
    onehot = tbuf[:, images].reshape(targets, LANES)[:, :CLASSES]
    offset = lax.dot_general(
        own_duals, onehot, nt_dims, precision=HIGH, preferred_element_type=jnp.float32
    )
    accl[...] = jnp.zeros_like(accl)
    accc[...] = jnp.zeros_like(accc)

    k_all().wait_recv()
    columns = jnp.concatenate([kbuf[d] for d in range(ndev)], axis=0)
    weight = jnp.dot(gram, columns, precision=HIGH, preferred_element_type=jnp.float32) - offset
    wide = (weight[:, None, :] * keep[None]).reshape(own_s * groups, targets)
    wexp[...] = jnp.dot(
        wide, spread, precision=HIGH, preferred_element_type=jnp.float32
    ).reshape(own_s, groups, LANES)

    def block_backward(owner, carry):
        level_terms = [[None] * PACK for _ in range(LAYERS)]
        channel_terms = [[None] * PACK for _ in range(CHANNELS)]

        def add(table, at, k, value):
            table[at][k] = value if table[at][k] is None else table[at][k] + value

        for gl in range(groups_own):
            g = owner * groups_own + gl
            upstream = [jnp.broadcast_to(wexp[:, pl.ds(g, 1), :], (own_s, SUB, LANES))] * PACK
            for layer in range(LAYERS - 1, -1, -1):
                passed = []
                for k in range(PACK):
                    add(level_terms, layer, k, upstream[k] * amp[g, layer, k])
                    passed.append(upstream[k] * ang[g, layer, k])
                upstream = box_sum(passed, mask)
            for channel in range(CHANNELS):
                for k in range(PACK):
                    image = tbuf[owner, (gl * CHANNELS + channel) * PACK + k]
                    add(channel_terms, channel, k, upstream[k] * image[None])
        for layer in range(LAYERS):
            for k in range(PACK):
                accl[layer, k] += level_terms[layer][k]
        for channel in range(CHANNELS):
            for k in range(PACK):
                accc[channel, k] += channel_terms[channel][k]
        return carry

    lax.fori_loop(0, nt, block_backward, 0)

    def over_images(v):
        v = v + pltpu.roll(v, 2 * SIDE, 2)
        return v + pltpu.roll(v, SIDE, 2)

    level_grad = None
    for layer in range(LAYERS - 1, -1, -1):
        scale = 9.0**layer / (2.0 * math.pi * 9.0 ** (LAYERS - 1 - layer))
        term = [
            over_images(accl[layer, k]) * (sroot[layer, 0, k] * scale) for k in range(PACK)
        ]
        if level_grad is not None:
            carried = box_sum(level_grad, mask)
            term = [t + c * (1.0 / 9.0) for t, c in zip(term, carried)]
        level_grad = term
    energy = [v * (2.0 / (9.0 * CHANNELS)) for v in box_sum(level_grad, mask)]
    for channel in range(CHANNELS):
        natural = None
        for k in range(PACK):
            value = over_images(accc[channel, k]) * (1.0 / (CHANNELS * 9.0**LAYERS))
            value = value + srep[channel, k] * energy[k]
            natural = value if natural is None else jnp.where(mask[4] == k, value, natural)
        flat[...] = natural
        for s in range(SUB):
            grad_ref[channel, s] = flat[:, s, :]

    pred[...] = jnp.dot(columns.T, duals, precision=HIGH, preferred_element_type=jnp.float32)
    residual_ref[...] = pred[pl.ds(ti * own_t, own_t), :] - own_onehot[:own_t, :CLASSES]

    for gl in range(groups_own):
        for way in range(2):
            onward = chip + 1 - 2 * way
            for h in range(chips):
                source = chip - (1 - 2 * way) * h

                @pl.when((source >= 0) & (source < chips) & (onward >= 0) & (onward < chips))
                def _():
                    plane_copy(source, gl, way, onward).wait_send()

        for p in range(chips):
            part_copy(p, gl, core).wait_send()

    def drain_dual(step, carry):
        dual_copy(lax.rem(si + step, ns)).wait_send()
        return carry

    lax.fori_loop(1, ns, drain_dual, 0)

    k_all().wait_send()


def hand_over(residual_ref, grad_ref, residual_out, grad_out):
    residual_out[...] = residual_ref[...]
    grad_out[...] = grad_ref[...]


def shards(nt, ns, target_pool, target_index, target_labels, dual_weights, support_images):
    own_t = target_index.shape[0]
    own_s = support_images.shape[0]
    groups = nt * own_t // PACK
    images = own_t * CHANNELS
    chips = nt // 2
    ndev = nt * ns
    f32 = jnp.float32
    vmem = pl.BlockSpec(memory_space=pltpu.VMEM)
    smem = pl.BlockSpec(memory_space=pltpu.SMEM)
    dma = pltpu.SemaphoreType.DMA
    tile = (SUB, LANES)
    residual, grad = pl.pallas_call(
        functools.partial(kernel, nt, ns, own_t, own_s),
        out_shape=(
            jax.ShapeDtypeStruct((own_t, CLASSES), f32),
            jax.ShapeDtypeStruct((CHANNELS, SUB, own_s, LANES), f32),
        ),
        in_specs=[smem, smem, vmem, vmem, vmem],
        out_specs=(vmem, vmem),
        scratch_shapes=[
            pltpu.VMEM((nt, images + 1) + tile, f32),
            pltpu.VMEM((ns,) + dual_weights.shape, f32),
            pltpu.VMEM((ndev, own_s, nt * own_t), f32),
            pltpu.VMEM((CHANNELS, PACK, own_s) + tile, f32),
            pltpu.VMEM((LAYERS, 2, PACK, own_s) + tile, f32),
            pltpu.VMEM((LAYERS, 2, PACK) + tile, f32),
            pltpu.VMEM((groups, LAYERS, PACK, own_s) + tile, f32),
            pltpu.VMEM((groups, LAYERS, PACK, own_s) + tile, f32),
            pltpu.VMEM((own_s, groups, LANES), f32),
            pltpu.VMEM((own_s, groups, LANES), f32),
            pltpu.VMEM((LAYERS, PACK, own_s) + tile, f32),
            pltpu.VMEM((CHANNELS, PACK, own_s) + tile, f32),
            pltpu.VMEM((nt * own_t, CLASSES), f32),
            pltpu.VMEM((own_s,) + tile, f32),
            dma((2, chips, own_t // PACK)),
            dma((chips, own_t // PACK)),
            dma((chips, own_t // PACK)),
            dma((chips, own_t // PACK)),
            dma((ns,)),
            dma((ns,)),
            dma,
            dma,
            pltpu.SemaphoreType.REGULAR,
        ],
        compiler_params=pltpu.CompilerParams(collective_id=0, has_side_effects=True, vmem_limit_bytes=24 * 2**20),
    )(
        target_index,
        target_labels,
        target_pool.reshape(-1, SUB, CHANNELS, SUB, LANES).transpose(2, 0, 3, 1, 4),
        dual_weights,
        support_images.reshape(own_s, CHANNELS, SUB, LANES).transpose(1, 2, 0, 3),
    )
    residual, grad = pl.pallas_call(
        hand_over,
        out_shape=(
            jax.ShapeDtypeStruct(residual.shape, f32),
            jax.ShapeDtypeStruct(grad.shape, f32),
        ),
        in_specs=[vmem, vmem],
        out_specs=(vmem, vmem),
        compiler_params=pltpu.CompilerParams(vmem_limit_bytes=2**20),
    )(residual, grad)
    return (residual, grad.transpose(2, 0, 1, 3).reshape(support_images.shape))


def solution(mesh):
    in_specs = (
        P("tgt", None, None),
        P("tgt"),
        P("tgt"),
        P("sup", None),
        P(("sup", "tgt"), None, None),
    )
    out_specs = (P("tgt", None), P(("sup", "tgt"), None, None))
    body = functools.partial(shards, mesh.shape["tgt"], mesh.shape["sup"])
    return jax.shard_map(body, mesh=mesh, in_specs=in_specs, out_specs=out_specs, check_vma=False)
```

profile of v0, /device:TPU:0, one launch (start us, length us, event | category | flops | bytes accessed | tf_op | source)
XLA Modules:
  0.0 34.1 jit_solution(5095281154818372123)
XLA Ops:
  0.6 0.0 copy-start.3
  0.6 0.0 copy-start.4
  0.7 0.6 %copy-done.3 = s32[8]{0:T(128)S(1)} copy-done((s32[8]{0:T(128)S(1)}, s32[8]{0:T(128)}, u32[]{:S(2)}) %copy-start.3) | copy-done | bytes 56
  1.3 0.0 copy-done.4
  1.3 0.0 copy-start
  1.3 1.1 %copy-done = f32[64,3,1024]{2,0,1:T(8,128)S(1)} copy-done((f32[64,3,1024]{2,0,1:T(8,128)S(1)}, f32[64,3,1024]{2,0,1:T(8,128)}, u32[]{:S(2)}) %copy-start) | copy-done | bytes 786456
  2.4 0.0 copy-start.1
  2.4 0.8 %copy-done.1 = f32[4,3,1024]{2,0,1:T(4,128)S(1)} copy-done((f32[4,3,1024]{2,0,1:T(4,128)S(1)}, f32[4,3,1024]{2,0,1:T(4,128)}, u32[]{:S(2)}) %copy-start.1) | copy-done | bytes 49176
  3.2 0.0 copy-start.2
  3.2 0.7 %copy-done.2 = f32[32,100]{1,0:T(8,128)S(1)} copy-done((f32[32,100]{1,0:T(8,128)S(1)}, f32[32,100]{1,0:T(8,128)}, u32[]{:S(2)}) %copy-start.2) | copy-done | bytes 12824
  4.0 29.5 %shard_map.68 = (f32[8,100]{1,0:T(8,128)S(1)}, f32[3,8,4,128]{3,2,1,0:T(4,128)S(1)}) custom-call(s32[8]{0:T(128)S(1)} %copy-done.3, s32[8]{0:T(128)S(1)} %copy-done.4, f32[3,8,8,8,128]{4,3,2,1,0:T(8,128)S(1)} %bitcast.9, f32[32,100]{1,0:T(8,128)S(1)} %copy-done.2, f32[3,8,4,128]{3,2,1,0:T(4,128)S(1)} %bitcast.10), custom_call_target="tpu_custom_call" | custom-call | tf_op jit(solution)/shard_map/pallas_call | solution.py:485
  33.5 0.6 %shard_map.69 = (f32[8,100]{1,0:T(8,128)}, f32[3,8,4,128]{3,2,1,0:T(4,128)}) custom-call(f32[8,100]{1,0:T(8,128)S(1)} %get-tuple-element.6.residual_ref, f32[3,8,4,128]{3,2,1,0:T(4,128)S(1)} %get-tuple-element.7.grad_ref), custom_call_target="tpu_custom_call" | custom-call | tf_op jit(solution)/shard_map/pallas_call | solution.py:526
Async XLA Ops:
  0.6 0.7 %copy-start.3 = (s32[8]{0:T(128)S(1)}, s32[8]{0:T(128)}, u32[]{:S(2)}) copy-start(s32[8]{0:T(128)} %index_ref.1) | copy-start | bytes 100
  0.6 0.7 %copy-start.4 = (s32[8]{0:T(128)S(1)}, s32[8]{0:T(128)}, u32[]{:S(2)}) copy-start(s32[8]{0:T(128)} %label_ref.1) | copy-start | bytes 100
  1.3 1.1 %copy-start = (f32[64,3,1024]{2,0,1:T(8,128)S(1)}, f32[64,3,1024]{2,0,1:T(8,128)}, u32[]{:S(2)}) copy-start(f32[64,3,1024]{2,0,1:T(8,128)} %param.5) | copy-start | bytes 2359300
  2.4 0.8 %copy-start.1 = (f32[4,3,1024]{2,0,1:T(4,128)S(1)}, f32[4,3,1024]{2,0,1:T(4,128)}, u32[]{:S(2)}) copy-start(f32[4,3,1024]{2,0,1:T(4,128)} %param.9) | copy-start | bytes 147460
  3.2 0.7 %copy-start.2 = (f32[32,100]{1,0:T(8,128)S(1)}, f32[32,100]{1,0:T(8,128)}, u32[]{:S(2)}) copy-start(f32[32,100]{1,0:T(8,128)} %dual_ref.1) | copy-start | bytes 38404
where the time goes:
time: 34.4 us; the launch traced here: 34.1 us
  Pallas kernels  30.2 us (88%)
  local copies, waits for them, and re-layouts  3.3 us (10%)
  between operations  0.66 us (2%)
    pallas_call x1, Pallas kernels, shards(): pl.pallas_call(functools.partial(kernel, nt, ns, own_t, own_s), out_shape...  29.5 us
    unnamed x10, local copies, waits for them, and re-layouts  3.3 us

commit v1 on v0

v1 whole, which is shorter than its diff:
```python
import functools
import math

import jax
import jax.numpy as jnp
from jax import lax
from jax.experimental import pallas as pl
from jax.experimental.pallas import tpu as pltpu
from jax.sharding import PartitionSpec as P

CHANNELS = 3
SIDE = 32
CLASSES = 100
LAYERS = 3
PIXELS = 1024
BETA = 0.01
PACK = 4
SUB = 8
LANES = 128
MESH = pl.DeviceIdType.MESH
HIGH = lax.Precision.HIGHEST
ACOS = (
    1.5707956895,
    -0.2145428158,
    0.0881710453,
    -0.0459272047,
    0.0206200335,
    -0.0049111629,
)


def masks():
    lane = lax.broadcasted_iota(jnp.int32, (SUB, LANES), 1)
    row = lax.broadcasted_iota(jnp.int32, (SUB, LANES), 0)
    column = lane % SIDE
    return (column > 0, column < SIDE - 1, row > 0, row < SUB - 1, lane // SIDE)


def box_sum(maps, mask):
    right, left, down, up, _ = mask
    axis = maps[0].ndim - 1

    def across(v):
        return (
            v
            + jnp.where(right, pltpu.roll(v, 1, axis), 0.0)
            + jnp.where(left, pltpu.roll(v, LANES - 1, axis), 0.0)
        )

    before = jnp.where(down, pltpu.roll(maps[3], 1, axis - 1), 0.0)
    after = jnp.where(up, pltpu.roll(maps[0], SUB - 1, axis - 1), 0.0)
    low = maps[0] + maps[1]
    high = maps[2] + maps[3]
    return [across(v) for v in (before + low, low + maps[2], maps[1] + high, high + after)]


def interleave(images, mask):
    group = mask[4]
    out = []
    for k in range(PACK):
        total = None
        for m in range(PACK):
            shift = ((m - k) * SIDE) % LANES
            moved = images[m] if shift == 0 else pltpu.roll(images[m], shift, 1)
            total = moved if total is None else jnp.where(group == m, moved, total)
        out.append(total)
    return out


def replicate(image, mask):
    group = mask[4]
    out = []
    rolled = [image] + [pltpu.roll(image, SIDE * s, 1) for s in range(1, PACK)]
    for k in range(PACK):
        total = None
        for m in range(PACK):
            moved = rolled[(m - k) % PACK]
            total = moved if total is None else jnp.where(group == m, moved, total)
        out.append(total)
    return out


def levels_of(images, mask):
    energy = []
    for k in range(PACK):
        total = images[0][k] * images[0][k]
        for channel in range(1, CHANNELS):
            total = total + images[channel][k] * images[channel][k]
        energy.append(total * (1.0 / CHANNELS))
    levels = []
    current = energy
    for _ in range(LAYERS):
        current = [v * (1.0 / 9.0) + BETA for v in box_sum(current, mask)]
        levels.append(current)
    return levels


def split_rows(v):
    high = v.astype(jnp.bfloat16)
    rest = v - high.astype(jnp.float32)
    middle = rest.astype(jnp.bfloat16)
    low = (rest - middle.astype(jnp.float32)).astype(jnp.bfloat16)
    return jnp.concatenate([high, middle, low], axis=1)


def fold(a, b, keep, shift):
    return jnp.where(keep, a, b) + pltpu.roll(jnp.where(keep, b, a), shift, a.ndim - 1)


def kernel(
    nt, ns, own_t, own_s,
    index_hbm, label_hbm, pool_hbm, dual_hbm, support_hbm,
    residual_ref, grad_ref,
    index_ref, label_ref, pool_a, pool_b, pool_c, support_ref,
    tbuf, dbuf, lbuf, kbuf, srep, sroot, shalf, tlev, mid, held, amp, ang, unit, ksum, wexp, pred, flat,
    in_sem, plane_send, plane_recv, swap_send, part_send, part_recv,
    dual_send, dual_recv, label_send, label_recv, k_send, k_recv,
):
    ti = lax.axis_index("tgt")
    si = lax.axis_index("sup")
    pool_refs = (pool_a, pool_b, pool_c)
    chips = nt // 2
    chip = ti // 2
    core = ti % 2
    ndev = nt * ns
    me = si * nt + ti
    groups_own = own_t // PACK
    groups = nt * groups_own
    targets = nt * own_t
    mask = masks()
    share = 2 if groups_own % 2 == 0 and ns % 2 == 0 else 1
    beside = si + 1 - 2 * (si % 2)
    carried = [r * share + si % share for r in range(groups_own // share)]
    swapped = [r * share + (si + 1) % share for r in range(groups_own // share)] if share == 2 else []

    barrier = pltpu.get_barrier_semaphore()

    def others(action):
        for s in range(ns):
            for t in range(nt):
                pl.when((si != s) | (ti != t))(functools.partial(action, t, s))

    def greet(t, s):
        pl.semaphore_signal(barrier, inc=1, device_id=(t, s), device_id_type=MESH)

    for step in range(1, ns):
        greet(ti, lax.rem(si + step, ns))
    greet(chip * 2 + 1 - core, si)
    pl.when(chip > 0)(lambda: greet(ti - 2, si))
    pl.when(chip < chips - 1)(lambda: greet(ti + 2, si))

    def fetch(at, src, dst):
        return pltpu.make_async_copy(src, dst, in_sem.at[at])

    loads = [
        fetch(0, index_hbm, index_ref),
        fetch(1, label_hbm, label_ref),
        fetch(2, dual_hbm, dbuf.at[si]),
        fetch(3, support_hbm, support_ref),
    ] + [fetch(4 + c, pool_hbm.at[c], pool_refs[c]) for c in range(CHANNELS)]
    for at in (0, 4, 5, 6, 3, 2, 1):
        loads[at].start()

    def plane_copy(source_chip, gl, target_chip):
        part = tbuf.at[source_chip * 2 + core, gl]
        return pltpu.make_async_remote_copy(
            src_ref=part,
            dst_ref=part,
            send_sem=plane_send.at[jnp.where(target_chip > chip, 1, 0), source_chip, gl],
            recv_sem=plane_recv.at[source_chip, gl],
            device_id=(target_chip * 2 + core, si),
            device_id_type=MESH,
        )

    def swap_copy(source_chip, gl):
        part = tbuf.at[source_chip * 2 + core, gl]
        return pltpu.make_async_remote_copy(
            src_ref=part,
            dst_ref=part,
            send_sem=swap_send.at[source_chip, gl],
            recv_sem=plane_recv.at[source_chip, gl],
            device_id=(ti, beside),
            device_id_type=MESH,
        )

    def part_copy(source_chip, gl, side):
        part = tbuf.at[source_chip * 2 + side, gl]
        return pltpu.make_async_remote_copy(
            src_ref=part,
            dst_ref=part,
            send_sem=part_send.at[source_chip, gl],
            recv_sem=part_recv.at[source_chip, gl],
            device_id=(chip * 2 + 1 - core, si),
            device_id_type=MESH,
        )

    def dual_copy(s):
        return pltpu.make_async_remote_copy(
            src_ref=dbuf.at[si],
            dst_ref=dbuf.at[si],
            send_sem=dual_send.at[s],
            recv_sem=dual_recv.at[si],
            device_id=(ti, s),
            device_id_type=MESH,
        )

    def dual_arrival(s):
        return pltpu.make_async_remote_copy(
            src_ref=dbuf.at[s],
            dst_ref=dbuf.at[s],
            send_sem=dual_send.at[s],
            recv_sem=dual_recv.at[s],
            device_id=(ti, s),
            device_id_type=MESH,
        )

    def label_copy(t):
        return pltpu.make_async_remote_copy(
            src_ref=lbuf.at[ti],
            dst_ref=lbuf.at[ti],
            send_sem=label_send,
            recv_sem=label_recv,
            device_id=(t, si),
            device_id_type=MESH,
        )

    def label_all():
        slots = lbuf.at[pl.ds(0, nt - 1)]
        return pltpu.make_async_remote_copy(
            src_ref=slots,
            dst_ref=slots,
            send_sem=label_send,
            recv_sem=label_recv,
            device_id=(chip * 2 + 1 - core, si),
            device_id_type=MESH,
        )

    def k_copy(t, s):
        return pltpu.make_async_remote_copy(
            src_ref=kbuf.at[me],
            dst_ref=kbuf.at[me],
            send_sem=k_send,
            recv_sem=k_recv,
            device_id=(t, s),
            device_id_type=MESH,
        )

    def k_all():
        others_slots = kbuf.at[pl.ds(0, ndev - 1)]
        return pltpu.make_async_remote_copy(
            src_ref=others_slots,
            dst_ref=others_slots,
            send_sem=k_send,
            recv_sem=k_recv,
            device_id=(1 - core + chip * 2, si),
            device_id_type=MESH,
        )

    pool = pool_hbm.shape[1] * SUB
    loads[0].wait()
    picks = [lax.rem(index_ref[t], pool) for t in range(own_t)]
    for channel in range(CHANNELS):
        loads[4 + channel].wait()
        for gl in range(groups_own):
            natural = [
                pool_refs[channel][at // SUB, :, pl.ds(at % SUB, 1), :].reshape(SUB, LANES)
                for at in picks[gl * PACK : (gl + 1) * PACK]
            ]
            phases = interleave(natural, mask)
            for k in range(PACK):
                tbuf[ti, gl, channel * PACK + k] = phases[k]

    below = jnp.where(chip > 0, 1, 0)
    above = jnp.where(chip < chips - 1, 1, 0)
    pl.semaphore_wait(barrier, ns + below + above)

    def spread_out(source, gl, up, down):
        pl.when(up)(lambda: plane_copy(source, gl, chip + 1).start())
        pl.when(down)(lambda: plane_copy(source, gl, chip - 1).start())

    for gl in carried:
        spread_out(chip, gl, chip < chips - 1, chip > 0)
    for gl in range(groups_own):
        part_copy(chip, gl, core).start()

    loads[2].wait()

    def send_dual(step, carry):
        dual_copy(lax.rem(si + step, ns)).start()
        return carry

    lax.fori_loop(1, ns, send_dual, 0)

    loads[3].wait()
    for m in range(own_s):
        reps = []
        for channel in range(CHANNELS):
            phases = replicate(support_ref[channel, :, m, :], mask)
            reps.append(phases)
            for k in range(PACK):
                srep[channel, k, m] = phases[k]
        levels = levels_of(reps, mask)
        for layer in range(LAYERS):
            for k in range(PACK):
                inverse = lax.rsqrt(levels[layer][k])
                sroot[layer, 0, k, m] = inverse * (1.0 / 9.0**layer)
                sroot[layer, 1, k, m] = levels[layer][k] * inverse * (9.0**layer / math.pi)
                shalf[layer, k, m] = inverse * (1.0 / math.pi)

    def layer_map(g, layer, cross, inverse, root):
        mapped = []
        for k in range(PACK):
            x = cross[k] * (inverse[k][None] * sroot[layer, 0, k])
            size = jnp.abs(x) if layer == 0 else x
            gap = jnp.maximum(1.0 - size, 1e-20)
            rest = 1.0 + size
            half = gap * lax.rsqrt(gap)
            poly = size * (ACOS[-1] / math.pi) + ACOS[-2] / math.pi
            for term in ACOS[-3::-1]:
                poly = poly * size + term / math.pi
            near = half * poly
            slope = jnp.where(x >= 0.0, 1.0 - near, near) if layer == 0 else 1.0 - near
            sine = half * (rest * lax.rsqrt(rest))
            scaled = sine * root[k][None]
            amp[g, layer, k] = scaled
            ang[g, layer, k] = slope
            mapped.append(scaled * sroot[layer, 1, k] + slope * cross[k])
        return mapped

    def next_cross(mapped, layer):
        return [v + BETA * 9.0**layer for v in box_sum(mapped, mask)]

    def finish_group(g, at):
        cross = [mid[k] for k in range(PACK)]
        for layer in range(1, LAYERS):
            inverse = [tlev[at, layer - 1, 0, k] for k in range(PACK)]
            root = [tlev[at, layer - 1, 1, k] for k in range(PACK)]
            mapped = layer_map(g, layer, cross, inverse, root)
            if layer + 1 < LAYERS:
                cross = next_cross(mapped, layer + 1)
        total = (mapped[0] + mapped[1]) + (mapped[2] + mapped[3])
        ksum[:, pl.ds(g, 1), :] = jnp.sum(total, axis=1, keepdims=True)

    def begin_group(owner, gl, at):
        g = owner * groups_own + gl
        image = [
            [tbuf[owner, gl, channel * PACK + k] for k in range(PACK)]
            for channel in range(CHANNELS)
        ]
        levels = levels_of(image, mask)
        inverse = [[lax.rsqrt(levels[layer][k]) for k in range(PACK)] for layer in range(LAYERS)]
        root = [
            [levels[layer][k] * inverse[layer][k] for k in range(PACK)] for layer in range(LAYERS)
        ]
        for layer in range(1, LAYERS):
            for k in range(PACK):
                tlev[at, layer - 1, 0, k] = inverse[layer][k]
                tlev[at, layer - 1, 1, k] = root[layer][k]
        current = []
        for k in range(PACK):
            total = image[0][k][None] * srep[0, k]
            for channel in range(1, CHANNELS):
                total = total + image[channel][k][None] * srep[channel, k]
            current.append(total)
        cross = [v * (1.0 / 27.0) + BETA for v in box_sum(current, mask)]
        cross = next_cross(layer_map(g, 0, cross, inverse[0], root[0]), 1)
        for k in range(PACK):
            mid[k] = cross[k]

    def order(n):
        both = jnp.minimum(chip, chips - 1 - chip)
        h = (n + 1) // 2
        two_sided = jnp.where(n % 2 == 1, chip - h, chip + h)
        far = n - both
        one_sided = jnp.where(chip <= chips - 1 - chip, chip + far, chip - far)
        return jnp.where(n <= 2 * both, two_sided, one_sided)

    def place(slot):
        own = 2 * groups_own
        if share == 1:
            kind = lax.rem(slot, own)
            return slot // own, kind // groups_own, lax.rem(kind, groups_own), kind < groups_own
        reps = groups_own // 2
        r = lax.rem(slot, reps)
        step = slot // reps
        after = step - 6
        first = step < 4
        second = (step >= 4) & (step < 6)
        last = step >= 4 * chips - 2
        kind = lax.rem(after, 4)
        late = jnp.where(first, step % 2, jnp.where(second, 0, jnp.where(last, 1, kind % 2)))
        far = jnp.where(first, step // 2, jnp.where(second | last, step % 2, kind // 2))
        n = jnp.where(first, 0, jnp.where(second, 1, jnp.where(last, chips - 1, 2 + after // 4 - kind % 2)))
        return n, far, r * 2 + lax.rem(si + late, 2), late == 0

    def visit(slot, carry):
        before, at_before = carry
        n, far, gl, direct = place(slot)
        p = order(n)

        @pl.when((n > 0) & (far == 0))
        def _():
            plane_copy(p, gl, chip).wait_recv()

            @pl.when(direct)
            def _():
                spread_out(p, gl, (p < chip) & (chip < chips - 1), (p > chip) & (chip > 0))
                if share == 2:
                    swap_copy(p, gl).start()

            part_copy(p, gl, core).start()

        @pl.when(far == 1)
        def _():
            part_copy(p, gl, 1 - core).wait_recv()

        owner = p * 2 + jnp.where(far == 0, core, 1 - core)
        at = lax.rem(slot, 2)
        finish_group(before, at_before)
        begin_group(owner, gl, at)
        return owner * groups_own + gl, at

    for k in range(PACK):
        mid[k] = jnp.ones((own_s, SUB, LANES), jnp.float32)
        for layer in range(1, LAYERS):
            for which in range(2):
                tlev[1, layer - 1, which, k] = jnp.ones((SUB, LANES), jnp.float32)
    finish_group(*lax.fori_loop(0, groups, visit, (ti * groups_own, 1)))

    loads[1].wait()
    row = lax.broadcasted_iota(jnp.int32, (SUB, LANES), 0)
    lane = lax.broadcasted_iota(jnp.int32, (SUB, LANES), 1)
    line = lax.broadcasted_iota(jnp.int32, (1, LANES), 1)
    label = jnp.zeros((SUB, LANES), jnp.int32)
    labels = jnp.zeros((1, LANES), jnp.int32)
    for r in range(own_t):
        value = label_ref[r]
        label = jnp.where(row == r, value, label)
        labels = jnp.where(line == ti * own_t + r, value, labels)
    own_onehot = jnp.where(label == lane, 1.0, 0.0).astype(jnp.float32)
    lbuf[ti] = labels

    def send_label(step, carry):
        label_copy(lax.rem(ti + step, nt)).start()
        return carry

    lax.fori_loop(1, nt, send_label, 0)

    nt_dims = (((1,), (1,)), ((), ()))
    keep_g = lax.broadcasted_iota(jnp.int32, (groups, targets), 0)
    keep_t = lax.broadcasted_iota(jnp.int32, (groups, targets), 1)
    keep = jnp.where(keep_t // PACK == keep_g, 1.0, 0.0).astype(jnp.float32)
    wide_row = lax.broadcasted_iota(jnp.int32, (3 * LANES, targets), 0)
    wide_col = lax.broadcasted_iota(jnp.int32, (3 * LANES, targets), 1)
    gathers = jnp.where(wide_col % PACK == (wide_row % LANES) // SIDE, 1.0, 0.0).astype(jnp.bfloat16)
    lane_sums = jnp.dot(
        split_rows(ksum[...].reshape(own_s * groups, LANES)), gathers,
        preferred_element_type=jnp.float32,
    ) * (1.0 / (PIXELS * 9.0 ** (LAYERS - 1)))
    picked = jnp.sum(lane_sums.reshape(own_s, groups, targets) * keep[None], axis=1)
    kbuf[me] = picked

    others(lambda t, s: k_copy(t, s).start())

    part_s = 2 if own_s % 2 == 0 else own_s
    parts = own_s // part_s
    items = groups * parts

    def pair_stage(item, stage):
        item = jnp.clip(item, 0, items - 1)
        g = item // parts
        some = pl.ds((item % parts) * part_s, part_s)
        layer = LAYERS - 1 - stage
        term = [amp[g, layer, k, some] * shalf[layer, k, some] for k in range(PACK)]
        slope = [ang[g, layer, k, some] for k in range(PACK)]
        if stage > 0:
            term = [t * held[stage - 1, 0, k] + held[stage - 1, 1, k] for k, t in enumerate(term)]
            slope = [v * held[stage - 1, 0, k] for k, v in enumerate(slope)]
        level = box_sum(term, mask)
        passed = box_sum(slope, mask)
        if stage + 1 < LAYERS:
            for k in range(PACK):
                held[stage, 0, k] = passed[k]
                held[stage, 1, k] = level[k]
            return
        owner = g // groups_own
        gl = g % groups_own
        for channel in range(CHANNELS):
            for k in range(PACK):
                image = tbuf[owner, gl, channel * PACK + k]
                unit[g, channel, k, some] = (
                    passed[k] * image[None] + srep[channel, k, some] * level[k]
                )

    for stage in range(LAYERS - 1):
        for which in range(2):
            for k in range(PACK):
                held[stage, which, k] = jnp.zeros((part_s, SUB, LANES), jnp.float32)

    def pair_unit(step, carry):
        for stage in range(LAYERS - 1, -1, -1):
            pair_stage(step - stage, stage)
        return carry

    lax.fori_loop(0, items + LAYERS - 1, pair_unit, 0)

    def take_dual(step, carry):
        dual_arrival(lax.rem(si + step, ns)).wait_recv()
        return carry

    lax.fori_loop(1, ns, take_dual, 0)
    duals = dbuf[...].reshape(ns * dual_hbm.shape[0], CLASSES)
    own_duals = dbuf[si, pl.ds(ti * own_s, own_s), :]
    gram = lax.dot_general(
        own_duals, duals, nt_dims, precision=HIGH, preferred_element_type=jnp.float32
    )
    label_all().wait_recv()
    named = lbuf[0]
    for t in range(1, nt):
        named = named + lbuf[t]
    classes = lax.broadcasted_iota(jnp.int32, (CLASSES, targets), 0)
    onehot = jnp.where(classes == named[:, :targets], 1.0, 0.0).astype(jnp.float32)
    offset = jnp.dot(own_duals, onehot, precision=HIGH, preferred_element_type=jnp.float32)

    for gl in carried:
        for target, there in ((chip + 1, chip < chips - 1), (chip - 1, chip > 0)):
            pl.when(there)(functools.partial(lambda gl, target: plane_copy(chip, gl, target).wait_send(), gl, target))
    for gl in range(groups_own):
        part_copy(chip, gl, core).wait_send()

    def drain(n, carry):
        p = order(n)
        for gl in carried:
            pl.when((p < chip) & (chip < chips - 1))(
                functools.partial(lambda gl: plane_copy(p, gl, chip + 1).wait_send(), gl)
            )
            pl.when((p > chip) & (chip > 0))(
                functools.partial(lambda gl: plane_copy(p, gl, chip - 1).wait_send(), gl)
            )
            if share == 2:
                swap_copy(p, gl).wait_send()
        for gl in range(groups_own):
            part_copy(p, gl, core).wait_send()
        return carry

    lax.fori_loop(1, chips, drain, 0)

    def drain_dual(step, carry):
        dual_copy(lax.rem(si + step, ns)).wait_send()
        return carry

    lax.fori_loop(1, ns, drain_dual, 0)
    label_all().wait_send()
    k_all().wait_send()

    spread_row = lax.broadcasted_iota(jnp.int32, (3 * targets, LANES), 0)
    spread_lane = lax.broadcasted_iota(jnp.int32, (3 * targets, LANES), 1)
    spread = jnp.where(spread_row % PACK == spread_lane // SIDE, 1.0, 0.0).astype(jnp.bfloat16)

    k_all().wait_recv()
    columns = jnp.concatenate([kbuf[d] for d in range(ndev)], axis=0)
    weight = jnp.dot(gram, columns, precision=HIGH, preferred_element_type=jnp.float32) - offset
    weight = weight * (1.0 / (CHANNELS * 9.0**LAYERS))
    wide = (weight[:, None, :] * keep[None]).reshape(own_s * groups, targets)
    wexp[...] = jnp.dot(split_rows(wide), spread, preferred_element_type=jnp.float32)
    pred[...] = columns.T

    def gather_grad(first):
        pairs = [(channel, k) for channel in range(CHANNELS) for k in (first, first + 1)]

        def body(g, sums):
            w = [wexp[pl.ds(m * groups + g, SUB, stride=0), :] for m in range(own_s)]
            return tuple(
                tuple(total[m] + w[m] * unit[g, channel, k, m] for m in range(own_s))
                for total, (channel, k) in zip(sums, pairs)
            )

        zero = jnp.zeros((SUB, LANES), jnp.float32)
        sums = lax.fori_loop(0, groups, body, ((zero,) * own_s,) * len(pairs))
        return {pair: jnp.stack(total) for pair, total in zip(pairs, sums)}

    even = mask[4] % 2 == 0
    early = mask[4] < 2
    low = gather_grad(0)
    low = [fold(low[channel, 0], low[channel, 1], even, SIDE) for channel in range(CHANNELS)]
    high = gather_grad(2)
    high = [fold(high[channel, 2], high[channel, 3], even, SIDE) for channel in range(CHANNELS)]
    residual_ref[...] = jnp.dot(
        pred[pl.ds(ti * own_t, own_t), :], duals, precision=HIGH, preferred_element_type=jnp.float32
    ) - own_onehot[:own_t, :CLASSES]
    for channel in range(CHANNELS):
        flat[channel] = fold(low[channel], high[channel], early, 2 * SIDE)
        for s in range(SUB):
            grad_ref[channel, s] = flat[channel, :, s, :]


def hand_over(residual_ref, grad_ref, residual_out, grad_out):
    residual_out[...] = residual_ref[...]
    grad_out[...] = grad_ref[...]


def shards(nt, ns, target_pool, target_index, target_labels, dual_weights, support_images):
    own_t = target_index.shape[0]
    own_s = support_images.shape[0]
    groups_own = own_t // PACK
    groups = nt * groups_own
    chips = nt // 2
    ndev = nt * ns
    f32 = jnp.float32
    vmem = pl.BlockSpec(memory_space=pltpu.VMEM)
    hbm = pl.BlockSpec(memory_space=pltpu.HBM)
    dma = pltpu.SemaphoreType.DMA
    tile = (SUB, LANES)
    pool = target_pool.reshape(-1, SUB, CHANNELS, SUB, LANES).transpose(2, 0, 3, 1, 4)
    support = support_images.reshape(own_s, CHANNELS, SUB, LANES).transpose(1, 2, 0, 3)
    residual, grad = pl.pallas_call(
        functools.partial(kernel, nt, ns, own_t, own_s),
        out_shape=(
            jax.ShapeDtypeStruct((own_t, CLASSES), f32),
            jax.ShapeDtypeStruct((CHANNELS, SUB, own_s, LANES), f32),
        ),
        in_specs=[hbm] * 5,
        out_specs=(vmem, vmem),
        scratch_shapes=[
            pltpu.SMEM((own_t,), jnp.int32),
            pltpu.SMEM((own_t,), jnp.int32),
            *[pltpu.VMEM(pool.shape[1:], f32)] * CHANNELS,
            pltpu.VMEM(support.shape, f32),
            pltpu.VMEM((nt, groups_own, CHANNELS * PACK) + tile, f32),
            pltpu.VMEM((ns,) + dual_weights.shape, f32),
            pltpu.VMEM((nt, 1, LANES), jnp.int32),
            pltpu.VMEM((ndev, own_s, nt * own_t), f32),
            pltpu.VMEM((CHANNELS, PACK, own_s) + tile, f32),
            pltpu.VMEM((LAYERS, 2, PACK, own_s) + tile, f32),
            pltpu.VMEM((LAYERS, PACK, own_s) + tile, f32),
            pltpu.VMEM((2, LAYERS - 1, 2, PACK) + tile, f32),
            pltpu.VMEM((PACK, own_s) + tile, f32),
            pltpu.VMEM((LAYERS - 1, 2, PACK, 2 if own_s % 2 == 0 else own_s) + tile, f32),
            pltpu.VMEM((groups, LAYERS, PACK, own_s) + tile, f32),
            pltpu.VMEM((groups, LAYERS, PACK, own_s) + tile, f32),
            pltpu.VMEM((groups, CHANNELS, PACK, own_s) + tile, f32),
            pltpu.VMEM((own_s, groups, LANES), f32),
            pltpu.VMEM((own_s * groups, LANES), f32),
            pltpu.VMEM((nt * own_t, ns * dual_weights.shape[0]), f32),
            pltpu.VMEM((CHANNELS, own_s) + tile, f32),
            dma((4 + CHANNELS,)),
            dma((2, chips, groups_own)),
            dma((chips, groups_own)),
            dma((chips, groups_own)),
            dma((chips, groups_own)),
            dma((chips, groups_own)),
            dma((ns,)),
            dma((ns,)),
            dma,
            dma,
            dma,
            dma,
        ],
        compiler_params=pltpu.CompilerParams(
            collective_id=0, has_side_effects=True, vmem_limit_bytes=44 * 2**20
        ),
    )(*[
        pltpu.with_memory_space_constraint(v, pltpu.HBM)
        for v in (target_index, target_labels, pool, dual_weights, support)
    ])
    residual, grad = pl.pallas_call(
        hand_over,
        out_shape=(
            jax.ShapeDtypeStruct(residual.shape, f32),
            jax.ShapeDtypeStruct(grad.shape, f32),
        ),
        in_specs=[vmem, vmem],
        out_specs=(vmem, vmem),
        compiler_params=pltpu.CompilerParams(vmem_limit_bytes=2**20),
    )(residual, grad)
    return (residual, grad.transpose(2, 0, 1, 3).reshape(support_images.shape))


def solution(mesh):
    in_specs = (
        P("tgt", None, None),
        P("tgt"),
        P("tgt"),
        P("sup", None),
        P(("sup", "tgt"), None, None),
    )
    out_specs = (P("tgt", None), P(("sup", "tgt"), None, None))
    body = functools.partial(shards, mesh.shape["tgt"], mesh.shape["sup"])
    return jax.shard_map(body, mesh=mesh, in_specs=in_specs, out_specs=out_specs, check_vma=False)
```

time: 34.4 us -> 29.7 us (0.86)
  local copies, waits for them, and re-layouts: 3.3 us -> 0 us
  Pallas kernels: 30.2 us -> 28.6 us
    unnamed x10 -> x0, local copies, waits for them, and re-layouts: 3.3 us -> none
    pallas_call x1, Pallas kernels: 29.5 us -> 28 us  [shards(): pl.pallas_call(functools.partial(kernel, nt, ns, own_t, own_s), out_shape...]
where the time goes in v1:
time: 29.7 us; the launch traced here: 29.2 us
  Pallas kernels  28.6 us (96%)
  between operations  0.64 us (2%)
    pallas_call x1, Pallas kernels, shards(): pl.pallas_call(functools.partial(kernel, nt, ns, own_t, own_s), out_shape...  28 us
    pallas_call x1, Pallas kernels, shards(): pl.pallas_call(hand_over, out_shape=(jax.ShapeDtypeStruct(residual.shape,...  0.63 us

profile of v1, /device:TPU:0, one launch (start us, length us, event | category | flops | bytes accessed | tf_op | source)
XLA Modules:
  0.0 29.2 jit_solution(11660240485344277266)
XLA Ops:
  0.6 28.0 %shard_map.68 = (f32[8,100]{1,0:T(8,128)S(1)}, f32[3,8,4,128]{3,2,1,0:T(4,128)S(1)}) custom-call(s32[8]{0:T(128)} %index_hbm.1, s32[8]{0:T(128)} %label_hbm.1, f32[3,8,8,8,128]{4,3,2,1,0:T(8,128)} %bitcast.9, f32[32,100]{1,0:T(8,128)} %dual_hbm.1, f32[3,8,4,128]{3,2,1,0:T(4,128)} %bitcast.10), custom_call_target="tpu_custom_call" | custom-call | tf_op jit(solution)/shard_map/pallas_call | solution.py:616
  28.6 0.6 %shard_map.69 = (f32[8,100]{1,0:T(8,128)}, f32[3,8,4,128]{3,2,1,0:T(4,128)}) custom-call(f32[8,100]{1,0:T(8,128)S(1)} %get-tuple-element.6.residual_ref, f32[3,8,4,128]{3,2,1,0:T(4,128)S(1)} %get-tuple-element.7.grad_ref), custom_call_target="tpu_custom_call" | custom-call | tf_op jit(solution)/shard_map/pallas_call | solution.py:666

commit v2 on v1

--- a/solution.py
+++ b/solution.py
@@ -29,6 +29,12 @@
 )
 
 
+STRETCH = (-ACOS[-1] / math.pi) ** (2.0 / (2 * len(ACOS) - 1))
+MONIC = [
+    term / ACOS[-1] * STRETCH ** (len(ACOS) - 1 - power) for power, term in enumerate(ACOS)
+][:-1]
+
+
 def masks():
     lane = lax.broadcasted_iota(jnp.int32, (SUB, LANES), 1)
     row = lax.broadcasted_iota(jnp.int32, (SUB, LANES), 0)
@@ -52,6 +58,31 @@
     low = maps[0] + maps[1]
     high = maps[2] + maps[3]
     return [across(v) for v in (before + low, low + maps[2], maps[1] + high, high + after)]
+
+
+def vertical(maps, mask):
+    down, up = mask[2], mask[3]
+    axis = maps[0].ndim - 2
+    before = jnp.where(down, pltpu.roll(maps[3], 1, axis), 0.0)
+    after = jnp.where(up, pltpu.roll(maps[0], SUB - 1, axis), 0.0)
+    low = maps[0] + maps[1]
+    high = maps[2] + maps[3]
+    return [before + low, low + maps[2], maps[1] + high, high + after]
+
+
+def band_sum(maps, mask, band):
+    return across(vertical(maps, mask), band)
+
+
+def across(maps, band):
+    shape = maps[0].shape
+    rows = jnp.stack(maps).reshape(-1, LANES)
+    high = rows.astype(jnp.bfloat16)
+    low = (rows - high.astype(jnp.float32)).astype(jnp.bfloat16)
+    out = jnp.dot(
+        jnp.concatenate([high, low], axis=1), band[...], preferred_element_type=jnp.float32
+    ).reshape((len(maps),) + shape)
+    return [out[k] for k in range(len(maps))]
 
 
 def interleave(images, mask):
@@ -112,7 +143,7 @@
     index_hbm, label_hbm, pool_hbm, dual_hbm, support_hbm,
     residual_ref, grad_ref,
     index_ref, label_ref, pool_a, pool_b, pool_c, support_ref,
-    tbuf, dbuf, lbuf, kbuf, srep, sroot, shalf, tlev, mid, held, amp, ang, unit, ksum, wexp, pred, flat,
+    tbuf, dbuf, lbuf, kbuf, band, gathers, spread, keep, srep, sroot, shalf, tlev, mid, held, amp, ang, unit, ksum, wexp, pred, flat,
     in_sem, plane_send, plane_recv, swap_send, part_send, part_recv,
     dual_send, dual_recv, label_send, label_recv, k_send, k_recv,
 ):
@@ -130,9 +161,6 @@
     mask = masks()
     share = 2 if groups_own % 2 == 0 and ns % 2 == 0 else 1
     beside = si + 1 - 2 * (si % 2)
-    carried = [r * share + si % share for r in range(groups_own // share)]
-    swapped = [r * share + (si + 1) % share for r in range(groups_own // share)] if share == 2 else []
-
     barrier = pltpu.get_barrier_semaphore()
 
     def others(action):
@@ -146,8 +174,8 @@
     for step in range(1, ns):
         greet(ti, lax.rem(si + step, ns))
     greet(chip * 2 + 1 - core, si)
-    pl.when(chip > 0)(lambda: greet(ti - 2, si))
-    pl.when(chip < chips - 1)(lambda: greet(ti + 2, si))
+    for step in range(1, chips):
+        greet(lax.rem(ti + 2 * step, nt), si)
 
     def fetch(at, src, dst):
         return pltpu.make_async_copy(src, dst, in_sem.at[at])
@@ -158,7 +186,7 @@
         fetch(2, dual_hbm, dbuf.at[si]),
         fetch(3, support_hbm, support_ref),
     ] + [fetch(4 + c, pool_hbm.at[c], pool_refs[c]) for c in range(CHANNELS)]
-    for at in (0, 4, 5, 6, 3, 2, 1):
+    for at in (3, 0, 4, 5, 6, 2, 1):
         loads[at].start()
 
     def plane_copy(source_chip, gl, target_chip):
@@ -166,7 +194,7 @@
         return pltpu.make_async_remote_copy(
             src_ref=part,
             dst_ref=part,
-            send_sem=plane_send.at[jnp.where(target_chip > chip, 1, 0), source_chip, gl],
+            send_sem=plane_send.at[target_chip, gl],
             recv_sem=plane_recv.at[source_chip, gl],
             device_id=(target_chip * 2 + core, si),
             device_id_type=MESH,
@@ -255,6 +283,40 @@
             device_id=(1 - core + chip * 2, si),
             device_id_type=MESH,
         )
+
+    band_row = lax.broadcasted_iota(jnp.int32, (LANES, LANES), 0)
+    band_col = lax.broadcasted_iota(jnp.int32, (LANES, LANES), 1)
+    near = (jnp.abs(band_row - band_col) <= 1) & (band_row // SIDE == band_col // SIDE)
+    near = jnp.where(near, 1.0, 0.0).astype(jnp.bfloat16)
+    for part in range(2):
+        band[pl.ds(part * LANES, LANES), :] = near
+    wide_row = lax.broadcasted_iota(jnp.int32, (LANES, targets), 0)
+    wide_col = lax.broadcasted_iota(jnp.int32, (LANES, targets), 1)
+    into = jnp.where(wide_col % PACK == wide_row // SIDE, 1.0, 0.0).astype(jnp.bfloat16)
+    tall_row = lax.broadcasted_iota(jnp.int32, (targets, LANES), 0)
+    tall_col = lax.broadcasted_iota(jnp.int32, (targets, LANES), 1)
+    onto = jnp.where(tall_row % PACK == tall_col // SIDE, 1.0, 0.0).astype(jnp.bfloat16)
+    for part in range(3):
+        gathers[pl.ds(part * LANES, LANES), :] = into
+        spread[pl.ds(part * targets, targets), :] = onto
+    keep_g = lax.broadcasted_iota(jnp.int32, (groups, targets), 0)
+    keep_t = lax.broadcasted_iota(jnp.int32, (groups, targets), 1)
+    keep[...] = jnp.where(keep_t // PACK == keep_g, 1.0, 0.0).astype(jnp.float32)
+    loads[3].wait()
+    for m in range(own_s):
+        reps = []
+        for channel in range(CHANNELS):
+            phases = replicate(support_ref[channel, :, m, :], mask)
+            reps.append(phases)
+            for k in range(PACK):
+                srep[channel, k, m] = phases[k] * (1.0 / (9.0 * CHANNELS))
+        levels = levels_of(reps, mask)
+        for layer in range(LAYERS):
+            for k in range(PACK):
+                inverse = lax.rsqrt(levels[layer][k])
+                sroot[layer, 0, k, m] = inverse * (STRETCH / 9.0**layer)
+                sroot[layer, 1, k, m] = levels[layer][k] * inverse * (9.0**layer / (STRETCH * math.pi))
+                shalf[layer, k, m] = inverse * (9.0 * CHANNELS / (STRETCH * math.pi))
 
     pool = pool_hbm.shape[1] * SUB
     loads[0].wait()
@@ -270,16 +332,20 @@
             for k in range(PACK):
                 tbuf[ti, gl, channel * PACK + k] = phases[k]
 
-    below = jnp.where(chip > 0, 1, 0)
-    above = jnp.where(chip < chips - 1, 1, 0)
-    pl.semaphore_wait(barrier, ns + below + above)
-
-    def spread_out(source, gl, up, down):
-        pl.when(up)(lambda: plane_copy(source, gl, chip + 1).start())
-        pl.when(down)(lambda: plane_copy(source, gl, chip - 1).start())
-
-    for gl in carried:
-        spread_out(chip, gl, chip < chips - 1, chip > 0)
+    pl.semaphore_wait(barrier, ns + chips - 1)
+
+    def choice(h):
+        return lax.rem(si + h, groups_own)
+
+    def each_plane(action):
+        for h in range(0, groups_own, share):
+            for step in range(chips - 1, 0, -1):
+                for target in (chip + step, chip - step):
+                    pl.when((target >= 0) & (target < chips))(
+                        functools.partial(action, choice(h), target)
+                    )
+
+    each_plane(lambda gl, target: plane_copy(chip, gl, target).start())
     for gl in range(groups_own):
         part_copy(chip, gl, core).start()
 
@@ -290,36 +356,20 @@
         return carry
 
     lax.fori_loop(1, ns, send_dual, 0)
-
-    loads[3].wait()
-    for m in range(own_s):
-        reps = []
-        for channel in range(CHANNELS):
-            phases = replicate(support_ref[channel, :, m, :], mask)
-            reps.append(phases)
-            for k in range(PACK):
-                srep[channel, k, m] = phases[k]
-        levels = levels_of(reps, mask)
-        for layer in range(LAYERS):
-            for k in range(PACK):
-                inverse = lax.rsqrt(levels[layer][k])
-                sroot[layer, 0, k, m] = inverse * (1.0 / 9.0**layer)
-                sroot[layer, 1, k, m] = levels[layer][k] * inverse * (9.0**layer / math.pi)
-                shalf[layer, k, m] = inverse * (1.0 / math.pi)
 
     def layer_map(g, layer, cross, inverse, root):
         mapped = []
         for k in range(PACK):
             x = cross[k] * (inverse[k][None] * sroot[layer, 0, k])
             size = jnp.abs(x) if layer == 0 else x
-            gap = jnp.maximum(1.0 - size, 1e-20)
-            rest = 1.0 + size
+            gap = jnp.maximum(STRETCH - size, 1e-20)
+            rest = STRETCH + size
             half = gap * lax.rsqrt(gap)
-            poly = size * (ACOS[-1] / math.pi) + ACOS[-2] / math.pi
-            for term in ACOS[-3::-1]:
-                poly = poly * size + term / math.pi
-            near = half * poly
-            slope = jnp.where(x >= 0.0, 1.0 - near, near) if layer == 0 else 1.0 - near
+            poly = size + MONIC[-1]
+            for term in MONIC[-2::-1]:
+                poly = poly * size + term
+            bend = half * poly
+            slope = jnp.where(x >= 0.0, 1.0 + bend, 0.0 - bend) if layer == 0 else 1.0 + bend
             sine = half * (rest * lax.rsqrt(rest))
             scaled = sine * root[k][None]
             amp[g, layer, k] = scaled
@@ -328,20 +378,20 @@
         return mapped
 
     def next_cross(mapped, layer):
-        return [v + BETA * 9.0**layer for v in box_sum(mapped, mask)]
-
-    def finish_group(g, at):
-        cross = [mid[k] for k in range(PACK)]
+        return [v + BETA * 9.0**layer for v in band_sum(mapped, mask, band)]
+
+    def finish_group(g, at, j):
+        cross = [v + BETA * 9.0 for v in across([mid[j, k] for k in range(PACK)], band)]
         for layer in range(1, LAYERS):
-            inverse = [tlev[at, layer - 1, 0, k] for k in range(PACK)]
-            root = [tlev[at, layer - 1, 1, k] for k in range(PACK)]
+            inverse = [tlev[at, j, layer - 1, 0, k] for k in range(PACK)]
+            root = [tlev[at, j, layer - 1, 1, k] for k in range(PACK)]
             mapped = layer_map(g, layer, cross, inverse, root)
             if layer + 1 < LAYERS:
                 cross = next_cross(mapped, layer + 1)
         total = (mapped[0] + mapped[1]) + (mapped[2] + mapped[3])
         ksum[:, pl.ds(g, 1), :] = jnp.sum(total, axis=1, keepdims=True)
 
-    def begin_group(owner, gl, at):
+    def begin_group(owner, gl, at, j):
         g = owner * groups_own + gl
         image = [
             [tbuf[owner, gl, channel * PACK + k] for k in range(PACK)]
@@ -354,18 +404,18 @@
         ]
         for layer in range(1, LAYERS):
             for k in range(PACK):
-                tlev[at, layer - 1, 0, k] = inverse[layer][k]
-                tlev[at, layer - 1, 1, k] = root[layer][k]
+                tlev[at, j, layer - 1, 0, k] = inverse[layer][k]
+                tlev[at, j, layer - 1, 1, k] = root[layer][k]
         current = []
         for k in range(PACK):
             total = image[0][k][None] * srep[0, k]
             for channel in range(1, CHANNELS):
                 total = total + image[channel][k][None] * srep[channel, k]
             current.append(total)
-        cross = [v * (1.0 / 27.0) + BETA for v in box_sum(current, mask)]
-        cross = next_cross(layer_map(g, 0, cross, inverse[0], root[0]), 1)
+        cross = [v + BETA for v in band_sum(current, mask, band)]
+        summed = vertical(layer_map(g, 0, cross, inverse[0], root[0]), mask)
         for k in range(PACK):
-            mid[k] = cross[k]
+            mid[j, k] = summed[k]
 
     def order(n):
         both = jnp.minimum(chip, chips - 1 - chip)
@@ -375,57 +425,54 @@
         one_sided = jnp.where(chip <= chips - 1 - chip, chip + far, chip - far)
         return jnp.where(n <= 2 * both, two_sided, one_sided)
 
-    def place(slot):
-        own = 2 * groups_own
-        if share == 1:
-            kind = lax.rem(slot, own)
-            return slot // own, kind // groups_own, lax.rem(kind, groups_own), kind < groups_own
-        reps = groups_own // 2
-        r = lax.rem(slot, reps)
-        step = slot // reps
-        after = step - 6
-        first = step < 4
-        second = (step >= 4) & (step < 6)
-        last = step >= 4 * chips - 2
-        kind = lax.rem(after, 4)
-        late = jnp.where(first, step % 2, jnp.where(second, 0, jnp.where(last, 1, kind % 2)))
-        far = jnp.where(first, step // 2, jnp.where(second | last, step % 2, kind // 2))
-        n = jnp.where(first, 0, jnp.where(second, 1, jnp.where(last, chips - 1, 2 + after // 4 - kind % 2)))
-        return n, far, r * 2 + lax.rem(si + late, 2), late == 0
-
-    def visit(slot, carry):
-        before, at_before = carry
-        n, far, gl, direct = place(slot)
+    def block(before, old, at, fresh):
+        for j, g in enumerate(before):
+            finish_group(g, old, j)
+        for j, (owner, gl) in enumerate(fresh):
+            begin_group(owner, gl, at, j)
+        return tuple(owner * groups_own + gl for owner, gl in fresh)
+
+    def near_item(n, gl, direct):
         p = order(n)
-
-        @pl.when((n > 0) & (far == 0))
-        def _():
-            plane_copy(p, gl, chip).wait_recv()
-
-            @pl.when(direct)
-            def _():
-                spread_out(p, gl, (p < chip) & (chip < chips - 1), (p > chip) & (chip > 0))
-                if share == 2:
-                    swap_copy(p, gl).start()
-
-            part_copy(p, gl, core).start()
-
-        @pl.when(far == 1)
-        def _():
-            part_copy(p, gl, 1 - core).wait_recv()
-
-        owner = p * 2 + jnp.where(far == 0, core, 1 - core)
-        at = lax.rem(slot, 2)
-        finish_group(before, at_before)
-        begin_group(owner, gl, at)
-        return owner * groups_own + gl, at
-
-    for k in range(PACK):
-        mid[k] = jnp.ones((own_s, SUB, LANES), jnp.float32)
-        for layer in range(1, LAYERS):
-            for which in range(2):
-                tlev[1, layer - 1, which, k] = jnp.ones((SUB, LANES), jnp.float32)
-    finish_group(*lax.fori_loop(0, groups, visit, (ti * groups_own, 1)))
+        plane_copy(p, gl, chip).wait_recv()
+        if share == 2:
+            pl.when(direct)(lambda: swap_copy(p, gl).start())
+        part_copy(p, gl, core).start()
+        return p * 2 + core, gl
+
+    def far_item(n, gl):
+        p = order(n)
+        part_copy(p, gl, 1 - core).wait_recv()
+        return p * 2 + 1 - core, gl
+
+    slots = max(chips - 1, 1)
+    before = ()
+    last = slots - 1
+    own = [(side, h) for side in (0, 1) for h in range(groups_own)]
+    for first in range(0, len(own), 2):
+        fresh = [
+            far_item(0, choice(h)) if side else (ti, choice(h))
+            for side, h in own[first : first + 2]
+        ]
+        at = (first // 2 - groups_own) % slots
+        before = block(before, last, at, fresh)
+        last = at
+
+    def sweep(h, before):
+        gl = choice(h)
+        direct = h % 2 == 0
+        items = [(side, n) for side in (0, 1) for n in range(1, chips)]
+        for first in range(0, len(items), 2):
+            fresh = [
+                far_item(n, gl) if side else near_item(n, gl, direct)
+                for side, n in items[first : first + 2]
+            ]
+            at = first // 2
+            before = block(before, (at - 1) % slots, at, fresh)
+        return before
+
+    before = lax.fori_loop(0, groups_own, sweep, before)
+    block(before, slots - 1, 0, [])
 
     loads[1].wait()
     row = lax.broadcasted_iota(jnp.int32, (SUB, LANES), 0)
@@ -447,62 +494,47 @@
     lax.fori_loop(1, nt, send_label, 0)
 
     nt_dims = (((1,), (1,)), ((), ()))
-    keep_g = lax.broadcasted_iota(jnp.int32, (groups, targets), 0)
-    keep_t = lax.broadcasted_iota(jnp.int32, (groups, targets), 1)
-    keep = jnp.where(keep_t // PACK == keep_g, 1.0, 0.0).astype(jnp.float32)
-    wide_row = lax.broadcasted_iota(jnp.int32, (3 * LANES, targets), 0)
-    wide_col = lax.broadcasted_iota(jnp.int32, (3 * LANES, targets), 1)
-    gathers = jnp.where(wide_col % PACK == (wide_row % LANES) // SIDE, 1.0, 0.0).astype(jnp.bfloat16)
     lane_sums = jnp.dot(
-        split_rows(ksum[...].reshape(own_s * groups, LANES)), gathers,
+        split_rows(ksum[...].reshape(own_s * groups, LANES)), gathers[...],
         preferred_element_type=jnp.float32,
     ) * (1.0 / (PIXELS * 9.0 ** (LAYERS - 1)))
-    picked = jnp.sum(lane_sums.reshape(own_s, groups, targets) * keep[None], axis=1)
+    picked = jnp.sum(lane_sums.reshape(own_s, groups, targets) * keep[...][None], axis=1)
     kbuf[me] = picked
 
     others(lambda t, s: k_copy(t, s).start())
 
-    part_s = 2 if own_s % 2 == 0 else own_s
-    parts = own_s // part_s
-    items = groups * parts
-
-    def pair_stage(item, stage):
-        item = jnp.clip(item, 0, items - 1)
-        g = item // parts
-        some = pl.ds((item % parts) * part_s, part_s)
-        layer = LAYERS - 1 - stage
-        term = [amp[g, layer, k, some] * shalf[layer, k, some] for k in range(PACK)]
-        slope = [ang[g, layer, k, some] for k in range(PACK)]
-        if stage > 0:
-            term = [t * held[stage - 1, 0, k] + held[stage - 1, 1, k] for k, t in enumerate(term)]
-            slope = [v * held[stage - 1, 0, k] for k, v in enumerate(slope)]
-        level = box_sum(term, mask)
-        passed = box_sum(slope, mask)
-        if stage + 1 < LAYERS:
-            for k in range(PACK):
-                held[stage, 0, k] = passed[k]
-                held[stage, 1, k] = level[k]
-            return
+    held[...] = jnp.zeros_like(held)
+
+    def pair_unit(step, carry):
+        levels = across([held[0, at, k] for at in range(LAYERS) for k in range(PACK)], band)
+        passes = across([held[1, at, k] for at in range(LAYERS) for k in range(PACK)], band)
+
+        g = jnp.clip(step - LAYERS, 0, groups - 1)
         owner = g // groups_own
         gl = g % groups_own
+        last = (LAYERS - 1) * PACK
         for channel in range(CHANNELS):
             for k in range(PACK):
                 image = tbuf[owner, gl, channel * PACK + k]
-                unit[g, channel, k, some] = (
-                    passed[k] * image[None] + srep[channel, k, some] * level[k]
+                unit[g, channel, k] = (
+                    passes[last + k] * image[None] + srep[channel, k] * levels[last + k]
                 )
-
-    for stage in range(LAYERS - 1):
-        for which in range(2):
-            for k in range(PACK):
-                held[stage, which, k] = jnp.zeros((part_s, SUB, LANES), jnp.float32)
-
-    def pair_unit(step, carry):
-        for stage in range(LAYERS - 1, -1, -1):
-            pair_stage(step - stage, stage)
+        for at in range(LAYERS - 1, -1, -1):
+            g = jnp.clip(step - at, 0, groups - 1)
+            layer = LAYERS - 1 - at
+            term = [amp[g, layer, k] * shalf[layer, k] for k in range(PACK)]
+            slope = [ang[g, layer, k] for k in range(PACK)]
+            if at > 0:
+                start = (at - 1) * PACK
+                term = [t * passes[start + k] + levels[start + k] for k, t in enumerate(term)]
+                slope = [v * passes[start + k] for k, v in enumerate(slope)]
+            for k, v in enumerate(vertical(term, mask)):
+                held[0, at, k] = v
+            for k, v in enumerate(vertical(slope, mask)):
+                held[1, at, k] = v
         return carry
 
-    lax.fori_loop(0, items + LAYERS - 1, pair_unit, 0)
+    lax.fori_loop(0, groups + LAYERS, pair_unit, 0)
 
     def take_dual(step, carry):
         dual_arrival(lax.rem(si + step, ns)).wait_recv()
@@ -522,25 +554,16 @@
     onehot = jnp.where(classes == named[:, :targets], 1.0, 0.0).astype(jnp.float32)
     offset = jnp.dot(own_duals, onehot, precision=HIGH, preferred_element_type=jnp.float32)
 
-    for gl in carried:
-        for target, there in ((chip + 1, chip < chips - 1), (chip - 1, chip > 0)):
-            pl.when(there)(functools.partial(lambda gl, target: plane_copy(chip, gl, target).wait_send(), gl, target))
+    each_plane(lambda gl, target: plane_copy(chip, gl, target).wait_send())
     for gl in range(groups_own):
         part_copy(chip, gl, core).wait_send()
 
     def drain(n, carry):
         p = order(n)
-        for gl in carried:
-            pl.when((p < chip) & (chip < chips - 1))(
-                functools.partial(lambda gl: plane_copy(p, gl, chip + 1).wait_send(), gl)
-            )
-            pl.when((p > chip) & (chip > 0))(
-                functools.partial(lambda gl: plane_copy(p, gl, chip - 1).wait_send(), gl)
-            )
-            if share == 2:
-                swap_copy(p, gl).wait_send()
-        for gl in range(groups_own):
-            part_copy(p, gl, core).wait_send()
+        for h in range(groups_own):
+            if share == 2 and h % 2 == 0:
+                swap_copy(p, choice(h)).wait_send()
+            part_copy(p, choice(h), core).wait_send()
         return carry
 
     lax.fori_loop(1, chips, drain, 0)
@@ -552,44 +575,33 @@
     lax.fori_loop(1, ns, drain_dual, 0)
     label_all().wait_send()
     k_all().wait_send()
-
-    spread_row = lax.broadcasted_iota(jnp.int32, (3 * targets, LANES), 0)
-    spread_lane = lax.broadcasted_iota(jnp.int32, (3 * targets, LANES), 1)
-    spread = jnp.where(spread_row % PACK == spread_lane // SIDE, 1.0, 0.0).astype(jnp.bfloat16)
 
     k_all().wait_recv()
     columns = jnp.concatenate([kbuf[d] for d in range(ndev)], axis=0)
     weight = jnp.dot(gram, columns, precision=HIGH, preferred_element_type=jnp.float32) - offset
     weight = weight * (1.0 / (CHANNELS * 9.0**LAYERS))
-    wide = (weight[:, None, :] * keep[None]).reshape(own_s * groups, targets)
-    wexp[...] = jnp.dot(split_rows(wide), spread, preferred_element_type=jnp.float32)
+    wide = (weight[:, None, :] * keep[...][None]).reshape(own_s * groups, targets)
+    wexp[...] = jnp.dot(split_rows(wide), spread[...], preferred_element_type=jnp.float32)
     pred[...] = columns.T
-
-    def gather_grad(first):
-        pairs = [(channel, k) for channel in range(CHANNELS) for k in (first, first + 1)]
-
-        def body(g, sums):
-            w = [wexp[pl.ds(m * groups + g, SUB, stride=0), :] for m in range(own_s)]
-            return tuple(
-                tuple(total[m] + w[m] * unit[g, channel, k, m] for m in range(own_s))
-                for total, (channel, k) in zip(sums, pairs)
-            )
-
-        zero = jnp.zeros((SUB, LANES), jnp.float32)
-        sums = lax.fori_loop(0, groups, body, ((zero,) * own_s,) * len(pairs))
-        return {pair: jnp.stack(total) for pair, total in zip(pairs, sums)}
 
     even = mask[4] % 2 == 0
     early = mask[4] < 2
-    low = gather_grad(0)
-    low = [fold(low[channel, 0], low[channel, 1], even, SIDE) for channel in range(CHANNELS)]
-    high = gather_grad(2)
-    high = [fold(high[channel, 2], high[channel, 3], even, SIDE) for channel in range(CHANNELS)]
+    for m in range(own_s):
+        sums = [[None] * PACK for _ in range(CHANNELS)]
+        for g in range(groups):
+            w = wexp[pl.ds(m * groups + g, SUB, stride=0), :]
+            for channel in range(CHANNELS):
+                for k in range(PACK):
+                    value = w * unit[g, channel, k, m]
+                    sums[channel][k] = value if g == 0 else sums[channel][k] + value
+        for channel in range(CHANNELS):
+            low = fold(sums[channel][0], sums[channel][1], even, SIDE)
+            high = fold(sums[channel][2], sums[channel][3], even, SIDE)
+            flat[channel, m] = fold(low, high, early, 2 * SIDE)
     residual_ref[...] = jnp.dot(
         pred[pl.ds(ti * own_t, own_t), :], duals, precision=HIGH, preferred_element_type=jnp.float32
     ) - own_onehot[:own_t, :CLASSES]
     for channel in range(CHANNELS):
-        flat[channel] = fold(low[channel], high[channel], early, 2 * SIDE)
         for s in range(SUB):
             grad_ref[channel, s] = flat[channel, :, s, :]
 
@@ -630,12 +642,16 @@
             pltpu.VMEM((ns,) + dual_weights.shape, f32),
             pltpu.VMEM((nt, 1, LANES), jnp.int32),
             pltpu.VMEM((ndev, own_s, nt * own_t), f32),
+            pltpu.VMEM((2 * LANES, LANES), jnp.bfloat16),
+            pltpu.VMEM((3 * LANES, nt * own_t), jnp.bfloat16),
+            pltpu.VMEM((3 * nt * own_t, LANES), jnp.bfloat16),
+            pltpu.VMEM((groups, nt * own_t), f32),
             pltpu.VMEM((CHANNELS, PACK, own_s) + tile, f32),
             pltpu.VMEM((LAYERS, 2, PACK, own_s) + tile, f32),
             pltpu.VMEM((LAYERS, PACK, own_s) + tile, f32),
-            pltpu.VMEM((2, LAYERS - 1, 2, PACK) + tile, f32),
-            pltpu.VMEM((PACK, own_s) + tile, f32),
-            pltpu.VMEM((LAYERS - 1, 2, PACK, 2 if own_s % 2 == 0 else own_s) + tile, f32),
+            pltpu.VMEM((max(chips - 1, 1), 2, LAYERS - 1, 2, PACK) + tile, f32),
+            pltpu.VMEM((2, PACK, own_s) + tile, f32),
+            pltpu.VMEM((2, LAYERS, PACK, own_s) + tile, f32),
             pltpu.VMEM((groups, LAYERS, PACK, own_s) + tile, f32),
             pltpu.VMEM((groups, LAYERS, PACK, own_s) + tile, f32),
             pltpu.VMEM((groups, CHANNELS, PACK, own_s) + tile, f32),
@@ -644,7 +660,7 @@
             pltpu.VMEM((nt * own_t, ns * dual_weights.shape[0]), f32),
             pltpu.VMEM((CHANNELS, own_s) + tile, f32),
             dma((4 + CHANNELS,)),
-            dma((2, chips, groups_own)),
+            dma((chips, groups_own)),
             dma((chips, groups_own)),
             dma((chips, groups_own)),
             dma((chips, groups_own)),

time: 29.7 us -> 25.1 us (0.85)
  Pallas kernels: 28.6 us -> 24.2 us
    pallas_call x1, Pallas kernels: 28 us -> 23.6 us  [shards(): pl.pallas_call(functools.partial(kernel, nt, ns, own_t, own_s), out_shape...]
where the time goes in v2:
time: 25.1 us; the launch traced here: 24.8 us
  Pallas kernels  24.2 us (96%)
  between operations  0.64 us (3%)
    pallas_call x1, Pallas kernels, shards(): pl.pallas_call(functools.partial(kernel, nt, ns, own_t, own_s), out_shape...  23.6 us
    pallas_call x1, Pallas kernels, shards(): pl.pallas_call(hand_over, out_shape=(jax.ShapeDtypeStruct(residual.shape,...  0.63 us

profile of v2, /device:TPU:0, one launch (start us, length us, event | category | flops | bytes accessed | tf_op | source)
XLA Modules:
  0.0 24.8 jit_solution(12353896066835208422)
XLA Ops:
  0.6 23.6 %shard_map.68 = (f32[8,100]{1,0:T(8,128)S(1)}, f32[3,8,4,128]{3,2,1,0:T(4,128)S(1)}) custom-call(s32[8]{0:T(128)} %index_hbm.1, s32[8]{0:T(128)} %label_hbm.1, f32[3,8,8,8,128]{4,3,2,1,0:T(8,128)} %bitcast.9, f32[32,100]{1,0:T(8,128)} %dual_hbm.1, f32[3,8,4,128]{3,2,1,0:T(4,128)} %bitcast.10), custom_call_target="tpu_custom_call" | custom-call | tf_op jit(solution)/shard_map/pallas_call | solution.py:628
  24.2 0.6 %shard_map.69 = (f32[8,100]{1,0:T(8,128)}, f32[3,8,4,128]{3,2,1,0:T(4,128)}) custom-call(f32[8,100]{1,0:T(8,128)S(1)} %get-tuple-element.6.residual_ref, f32[3,8,4,128]{3,2,1,0:T(4,128)S(1)} %get-tuple-element.7.grad_ref), custom_call_target="tpu_custom_call" | custom-call | tf_op jit(solution)/shard_map/pallas_call | solution.py:682

commit v3 on v2

--- a/solution.py
+++ b/solution.py
@@ -163,11 +163,6 @@
     beside = si + 1 - 2 * (si % 2)
     barrier = pltpu.get_barrier_semaphore()
 
-    def others(action):
-        for s in range(ns):
-            for t in range(nt):
-                pl.when((si != s) | (ti != t))(functools.partial(action, t, s))
-
     def greet(t, s):
         pl.semaphore_signal(barrier, inc=1, device_id=(t, s), device_id_type=MESH)
 
@@ -186,7 +181,7 @@
         fetch(2, dual_hbm, dbuf.at[si]),
         fetch(3, support_hbm, support_ref),
     ] + [fetch(4 + c, pool_hbm.at[c], pool_refs[c]) for c in range(CHANNELS)]
-    for at in (3, 0, 4, 5, 6, 2, 1):
+    for at in (0, 4, 5, 6, 3, 2, 1):
         loads[at].start()
 
     def plane_copy(source_chip, gl, target_chip):
@@ -194,7 +189,7 @@
         return pltpu.make_async_remote_copy(
             src_ref=part,
             dst_ref=part,
-            send_sem=plane_send.at[target_chip, gl],
+            send_sem=plane_send,
             recv_sem=plane_recv.at[source_chip, gl],
             device_id=(target_chip * 2 + core, si),
             device_id_type=MESH,
@@ -205,7 +200,7 @@
         return pltpu.make_async_remote_copy(
             src_ref=part,
             dst_ref=part,
-            send_sem=swap_send.at[source_chip, gl],
+            send_sem=swap_send,
             recv_sem=plane_recv.at[source_chip, gl],
             device_id=(ti, beside),
             device_id_type=MESH,
@@ -216,7 +211,7 @@
         return pltpu.make_async_remote_copy(
             src_ref=part,
             dst_ref=part,
-            send_sem=part_send.at[source_chip, gl],
+            send_sem=part_send,
             recv_sem=part_recv.at[source_chip, gl],
             device_id=(chip * 2 + 1 - core, si),
             device_id_type=MESH,
@@ -226,19 +221,20 @@
         return pltpu.make_async_remote_copy(
             src_ref=dbuf.at[si],
             dst_ref=dbuf.at[si],
-            send_sem=dual_send.at[s],
-            recv_sem=dual_recv.at[si],
+            send_sem=dual_send,
+            recv_sem=dual_recv,
             device_id=(ti, s),
             device_id_type=MESH,
         )
 
-    def dual_arrival(s):
-        return pltpu.make_async_remote_copy(
-            src_ref=dbuf.at[s],
-            dst_ref=dbuf.at[s],
-            send_sem=dual_send.at[s],
-            recv_sem=dual_recv.at[s],
-            device_id=(ti, s),
+    def dual_all():
+        slots = dbuf.at[pl.ds(0, ns - 1)]
+        return pltpu.make_async_remote_copy(
+            src_ref=slots,
+            dst_ref=slots,
+            send_sem=dual_send,
+            recv_sem=dual_recv,
+            device_id=(ti, lax.rem(si + 1, ns)),
             device_id_type=MESH,
         )
 
@@ -302,6 +298,53 @@
     keep_g = lax.broadcasted_iota(jnp.int32, (groups, targets), 0)
     keep_t = lax.broadcasted_iota(jnp.int32, (groups, targets), 1)
     keep[...] = jnp.where(keep_t // PACK == keep_g, 1.0, 0.0).astype(jnp.float32)
+    pool = pool_hbm.shape[1] * SUB
+    def choice(h):
+        return lax.rem(si + h, groups_own)
+
+    def take_group(gl):
+        picks = [lax.rem(index_ref[gl * PACK + i], pool) for i in range(PACK)]
+        for channel in range(CHANNELS):
+            natural = [
+                pool_refs[channel][at // SUB, :, pl.ds(at % SUB, 1), :].reshape(SUB, LANES)
+                for at in picks
+            ]
+            phases = interleave(natural, mask)
+            for k in range(PACK):
+                tbuf[ti, gl, channel * PACK + k] = phases[k]
+
+    loads[0].wait()
+    for channel in range(CHANNELS):
+        loads[4 + channel].wait()
+    for h in range(0, groups_own, share):
+        take_group(choice(h))
+
+    pl.semaphore_wait(barrier, ns + chips - 1)
+
+    def each_plane(action):
+        for h in range(0, groups_own, share):
+            for step in range(chips - 1, 0, -1):
+                for target in (chip + step, chip - step):
+                    pl.when((target >= 0) & (target < chips))(
+                        functools.partial(action, choice(h), target)
+                    )
+
+    each_plane(lambda gl, target: plane_copy(chip, gl, target).start())
+    for h in range(0, groups_own, share):
+        part_copy(chip, choice(h), core).start()
+    if share == 2:
+        for h in range(1, groups_own, share):
+            take_group(choice(h))
+            part_copy(chip, choice(h), core).start()
+
+    loads[2].wait()
+
+    def send_dual(step, carry):
+        dual_copy(lax.rem(si + step, ns)).start()
+        return carry
+
+    lax.fori_loop(1, ns, send_dual, 0)
+
     loads[3].wait()
     for m in range(own_s):
         reps = []
@@ -317,45 +360,6 @@
                 sroot[layer, 0, k, m] = inverse * (STRETCH / 9.0**layer)
                 sroot[layer, 1, k, m] = levels[layer][k] * inverse * (9.0**layer / (STRETCH * math.pi))
                 shalf[layer, k, m] = inverse * (9.0 * CHANNELS / (STRETCH * math.pi))
-
-    pool = pool_hbm.shape[1] * SUB
-    loads[0].wait()
-    picks = [lax.rem(index_ref[t], pool) for t in range(own_t)]
-    for channel in range(CHANNELS):
-        loads[4 + channel].wait()
-        for gl in range(groups_own):
-            natural = [
-                pool_refs[channel][at // SUB, :, pl.ds(at % SUB, 1), :].reshape(SUB, LANES)
-                for at in picks[gl * PACK : (gl + 1) * PACK]
-            ]
-            phases = interleave(natural, mask)
-            for k in range(PACK):
-                tbuf[ti, gl, channel * PACK + k] = phases[k]
-
-    pl.semaphore_wait(barrier, ns + chips - 1)
-
-    def choice(h):
-        return lax.rem(si + h, groups_own)
-
-    def each_plane(action):
-        for h in range(0, groups_own, share):
-            for step in range(chips - 1, 0, -1):
-                for target in (chip + step, chip - step):
-                    pl.when((target >= 0) & (target < chips))(
-                        functools.partial(action, choice(h), target)
-                    )
-
-    each_plane(lambda gl, target: plane_copy(chip, gl, target).start())
-    for gl in range(groups_own):
-        part_copy(chip, gl, core).start()
-
-    loads[2].wait()
-
-    def send_dual(step, carry):
-        dual_copy(lax.rem(si + step, ns)).start()
-        return carry
-
-    lax.fori_loop(1, ns, send_dual, 0)
 
     def layer_map(g, layer, cross, inverse, root):
         mapped = []
@@ -474,6 +478,19 @@
     before = lax.fori_loop(0, groups_own, sweep, before)
     block(before, slots - 1, 0, [])
 
+    nt_dims = (((1,), (1,)), ((), ()))
+    lane_sums = jnp.dot(
+        split_rows(ksum[...].reshape(own_s * groups, LANES)), gathers[...],
+        preferred_element_type=jnp.float32,
+    ) * (1.0 / (PIXELS * 9.0 ** (LAYERS - 1)))
+    picked = jnp.sum(lane_sums.reshape(own_s, groups, targets) * keep[...][None], axis=1)
+    kbuf[me] = picked
+
+    for dt in sorted(range(nt), key=lambda d: -min(d, nt - d)):
+        for ds in range(ns - 1, -1, -1):
+            if dt or ds:
+                k_copy(lax.rem(ti + dt, nt), lax.rem(si + ds, ns)).start()
+
     loads[1].wait()
     row = lax.broadcasted_iota(jnp.int32, (SUB, LANES), 0)
     lane = lax.broadcasted_iota(jnp.int32, (SUB, LANES), 1)
@@ -492,16 +509,6 @@
         return carry
 
     lax.fori_loop(1, nt, send_label, 0)
-
-    nt_dims = (((1,), (1,)), ((), ()))
-    lane_sums = jnp.dot(
-        split_rows(ksum[...].reshape(own_s * groups, LANES)), gathers[...],
-        preferred_element_type=jnp.float32,
-    ) * (1.0 / (PIXELS * 9.0 ** (LAYERS - 1)))
-    picked = jnp.sum(lane_sums.reshape(own_s, groups, targets) * keep[...][None], axis=1)
-    kbuf[me] = picked
-
-    others(lambda t, s: k_copy(t, s).start())
 
     held[...] = jnp.zeros_like(held)
 
@@ -536,11 +543,7 @@
 
     lax.fori_loop(0, groups + LAYERS, pair_unit, 0)
 
-    def take_dual(step, carry):
-        dual_arrival(lax.rem(si + step, ns)).wait_recv()
-        return carry
-
-    lax.fori_loop(1, ns, take_dual, 0)
+    dual_all().wait_recv()
     duals = dbuf[...].reshape(ns * dual_hbm.shape[0], CLASSES)
     own_duals = dbuf[si, pl.ds(ti * own_s, own_s), :]
     gram = lax.dot_general(
@@ -554,25 +557,22 @@
     onehot = jnp.where(classes == named[:, :targets], 1.0, 0.0).astype(jnp.float32)
     offset = jnp.dot(own_duals, onehot, precision=HIGH, preferred_element_type=jnp.float32)
 
-    each_plane(lambda gl, target: plane_copy(chip, gl, target).wait_send())
-    for gl in range(groups_own):
-        part_copy(chip, gl, core).wait_send()
-
-    def drain(n, carry):
-        p = order(n)
-        for h in range(groups_own):
-            if share == 2 and h % 2 == 0:
-                swap_copy(p, choice(h)).wait_send()
-            part_copy(p, choice(h), core).wait_send()
-        return carry
-
-    lax.fori_loop(1, chips, drain, 0)
-
-    def drain_dual(step, carry):
-        dual_copy(lax.rem(si + step, ns)).wait_send()
-        return carry
-
-    lax.fori_loop(1, ns, drain_dual, 0)
+    def sent(sem, count, width):
+        part = tbuf.at[pl.ds(0, count), pl.ds(0, width)]
+        pltpu.make_async_remote_copy(
+            src_ref=part,
+            dst_ref=part,
+            send_sem=sem,
+            recv_sem=plane_recv.at[chip, 0],
+            device_id=(chip * 2 + 1 - core, si),
+            device_id_type=MESH,
+        ).wait_send()
+
+    sent(plane_send, chips - 1, groups_own // share)
+    if share == 2:
+        sent(swap_send, chips - 1, groups_own // share)
+    sent(part_send, chips, groups_own)
+    dual_all().wait_send()
     label_all().wait_send()
     k_all().wait_send()
 
@@ -660,13 +660,13 @@
             pltpu.VMEM((nt * own_t, ns * dual_weights.shape[0]), f32),
             pltpu.VMEM((CHANNELS, own_s) + tile, f32),
             dma((4 + CHANNELS,)),
+            dma,
             dma((chips, groups_own)),
+            dma,
+            dma,
             dma((chips, groups_own)),
-            dma((chips, groups_own)),
-            dma((chips, groups_own)),
-            dma((chips, groups_own)),
-            dma((ns,)),
-            dma((ns,)),
+            dma,
+            dma,
             dma,
             dma,
             dma,

time: 25.1 us -> 24.6 us (0.980)
  Pallas kernels: 24.2 us -> 23.7 us
    pallas_call x1, Pallas kernels: 23.6 us -> 23.1 us  [shards(): pl.pallas_call(functools.partial(kernel, nt, ns, own_t, own_s), out_shape...]
where the time goes in v3:
time: 24.6 us; the launch traced here: 24.3 us
  Pallas kernels  23.7 us (96%)
  between operations  0.64 us (3%)
    pallas_call x1, Pallas kernels, shards(): pl.pallas_call(functools.partial(kernel, nt, ns, own_t, own_s), out_shape...  23.1 us
    pallas_call x1, Pallas kernels, shards(): pl.pallas_call(hand_over, out_shape=(jax.ShapeDtypeStruct(residual.shape,...  0.63 us

profile of v3, /device:TPU:0, one launch (start us, length us, event | category | flops | bytes accessed | tf_op | source)
XLA Modules:
  0.0 24.3 jit_solution(10698419612874297979)
XLA Ops:
  0.6 23.1 %shard_map.68 = (f32[8,100]{1,0:T(8,128)S(1)}, f32[3,8,4,128]{3,2,1,0:T(4,128)S(1)}) custom-call(s32[8]{0:T(128)} %index_hbm.1, s32[8]{0:T(128)} %label_hbm.1, f32[3,8,8,8,128]{4,3,2,1,0:T(8,128)} %bitcast.9, f32[32,100]{1,0:T(8,128)} %dual_hbm.1, f32[3,8,4,128]{3,2,1,0:T(4,128)} %bitcast.10), custom_call_target="tpu_custom_call" | custom-call | tf_op jit(solution)/shard_map/pallas_call | solution.py:628
  23.7 0.6 %shard_map.69 = (f32[8,100]{1,0:T(8,128)}, f32[3,8,4,128]{3,2,1,0:T(4,128)}) custom-call(f32[8,100]{1,0:T(8,128)S(1)} %get-tuple-element.6.residual_ref, f32[3,8,4,128]{3,2,1,0:T(4,128)S(1)} %get-tuple-element.7.grad_ref), custom_call_target="tpu_custom_call" | custom-call | tf_op jit(solution)/shard_map/pallas_call | solution.py:682

commit v4 on v3

--- a/solution.py
+++ b/solution.py
@@ -124,6 +124,11 @@
         current = [v * (1.0 / 9.0) + BETA for v in box_sum(current, mask)]
         levels.append(current)
     return levels
+
+
+def sharing(targets, own_s):
+    per = max(LANES // targets, 1)
+    return per if LANES % targets == 0 and own_s % per == 0 else 1
 
 
 def split_rows(v):
@@ -158,6 +163,7 @@
     groups_own = own_t // PACK
     groups = nt * groups_own
     targets = nt * own_t
+    per = sharing(targets, own_s)
     mask = masks()
     share = 2 if groups_own % 2 == 0 and ns % 2 == 0 else 1
     beside = si + 1 - 2 * (si % 2)
@@ -286,8 +292,8 @@
     near = jnp.where(near, 1.0, 0.0).astype(jnp.bfloat16)
     for part in range(2):
         band[pl.ds(part * LANES, LANES), :] = near
-    wide_row = lax.broadcasted_iota(jnp.int32, (LANES, targets), 0)
-    wide_col = lax.broadcasted_iota(jnp.int32, (LANES, targets), 1)
+    wide_row = lax.broadcasted_iota(jnp.int32, (LANES, per * targets), 0)
+    wide_col = lax.broadcasted_iota(jnp.int32, (LANES, per * targets), 1)
     into = jnp.where(wide_col % PACK == wide_row // SIDE, 1.0, 0.0).astype(jnp.bfloat16)
     tall_row = lax.broadcasted_iota(jnp.int32, (targets, LANES), 0)
     tall_col = lax.broadcasted_iota(jnp.int32, (targets, LANES), 1)
@@ -295,9 +301,9 @@
     for part in range(3):
         gathers[pl.ds(part * LANES, LANES), :] = into
         spread[pl.ds(part * targets, targets), :] = onto
-    keep_g = lax.broadcasted_iota(jnp.int32, (groups, targets), 0)
-    keep_t = lax.broadcasted_iota(jnp.int32, (groups, targets), 1)
-    keep[...] = jnp.where(keep_t // PACK == keep_g, 1.0, 0.0).astype(jnp.float32)
+    keep_g = lax.broadcasted_iota(jnp.int32, (groups, per * targets), 0)
+    keep_t = lax.broadcasted_iota(jnp.int32, (groups, per * targets), 1)
+    keep[...] = jnp.where(keep_t % targets // PACK == keep_g, 1.0, 0.0).astype(jnp.float32)
     pool = pool_hbm.shape[1] * SUB
     def choice(h):
         return lax.rem(si + h, groups_own)
@@ -483,8 +489,13 @@
         split_rows(ksum[...].reshape(own_s * groups, LANES)), gathers[...],
         preferred_element_type=jnp.float32,
     ) * (1.0 / (PIXELS * 9.0 ** (LAYERS - 1)))
-    picked = jnp.sum(lane_sums.reshape(own_s, groups, targets) * keep[...][None], axis=1)
-    kbuf[me] = picked
+    picked = jnp.sum(lane_sums.reshape(own_s, groups, per * targets) * keep[...][None], axis=1)
+    half = lax.broadcasted_iota(jnp.int32, (1, per * targets), 1) // targets
+    for r in range(own_s // per):
+        packed = picked[r * per : r * per + 1]
+        for h in range(1, per):
+            packed = jnp.where(half == h, picked[r * per + h : r * per + h + 1], packed)
+        kbuf[me, pl.ds(r, 1), :] = packed
 
     for dt in sorted(range(nt), key=lambda d: -min(d, nt - d)):
         for ds in range(ns - 1, -1, -1):
@@ -510,44 +521,72 @@
 
     lax.fori_loop(1, nt, send_label, 0)
 
-    held[...] = jnp.zeros_like(held)
-
-    def pair_unit(step, carry):
-        levels = across([held[0, at, k] for at in range(LAYERS) for k in range(PACK)], band)
-        passes = across([held[1, at, k] for at in range(LAYERS) for k in range(PACK)], band)
-
-        g = jnp.clip(step - LAYERS, 0, groups - 1)
-        owner = g // groups_own
-        gl = g % groups_own
-        last = (LAYERS - 1) * PACK
-        for channel in range(CHANNELS):
-            for k in range(PACK):
-                image = tbuf[owner, gl, channel * PACK + k]
-                unit[g, channel, k] = (
-                    passes[last + k] * image[None] + srep[channel, k] * levels[last + k]
-                )
-        for at in range(LAYERS - 1, -1, -1):
-            g = jnp.clip(step - at, 0, groups - 1)
+    def pair_step(step, stages):
+        ready = [at - 1 for at in stages if at > 0]
+        levels, passes = [
+            dict(zip(
+                [(at, k) for at in ready for k in range(PACK)],
+                across([held[which, at, k] for at in ready for k in range(PACK)], band)
+                if ready else [],
+            ))
+            for which in range(2)
+        ]
+        for at in sorted(stages, reverse=True):
+            g = step - at
+            if at == LAYERS:
+                owner = g // groups_own
+                gl = g % groups_own
+                for channel in range(CHANNELS):
+                    for k in range(PACK):
+                        image = tbuf[owner, gl, channel * PACK + k]
+                        unit[g, channel, k] = (
+                            passes[at - 1, k] * image[None] + srep[channel, k] * levels[at - 1, k]
+                        )
+                continue
             layer = LAYERS - 1 - at
             term = [amp[g, layer, k] * shalf[layer, k] for k in range(PACK)]
             slope = [ang[g, layer, k] for k in range(PACK)]
             if at > 0:
-                start = (at - 1) * PACK
-                term = [t * passes[start + k] + levels[start + k] for k, t in enumerate(term)]
-                slope = [v * passes[start + k] for k, v in enumerate(slope)]
+                term = [t * passes[at - 1, k] + levels[at - 1, k] for k, t in enumerate(term)]
+                slope = [v * passes[at - 1, k] for k, v in enumerate(slope)]
             for k, v in enumerate(vertical(term, mask)):
                 held[0, at, k] = v
             for k, v in enumerate(vertical(slope, mask)):
                 held[1, at, k] = v
+
+    span = 2
+    whole = max(groups - LAYERS, 0) // span
+
+    def pair_unit(trip, carry):
+        for extra in range(span):
+            pair_step(LAYERS + trip * span + extra, range(LAYERS + 1))
         return carry
 
-    lax.fori_loop(0, groups + LAYERS, pair_unit, 0)
+    for step in range(min(LAYERS, groups)):
+        pair_step(step, range(step + 1))
+    lax.fori_loop(0, whole, pair_unit, 0)
+    for step in range(LAYERS + whole * span, groups):
+        pair_step(step, range(LAYERS + 1))
+    for step in range(groups, groups + LAYERS):
+        pair_step(step, range(step - groups + 1, LAYERS + 1))
 
     dual_all().wait_recv()
-    duals = dbuf[...].reshape(ns * dual_hbm.shape[0], CLASSES)
+    rows = dual_hbm.shape[0] // per
+
+    def dual_rows(h):
+        if per == 1:
+            return dbuf[...].reshape(ns * rows, CLASSES)
+        return jnp.concatenate([dbuf[s, pl.ds(h, rows, stride=per), :] for s in range(ns)], axis=0)
+
     own_duals = dbuf[si, pl.ds(ti * own_s, own_s), :]
-    gram = lax.dot_general(
-        own_duals, duals, nt_dims, precision=HIGH, preferred_element_type=jnp.float32
+    gram = jnp.concatenate(
+        [
+            lax.dot_general(
+                own_duals, dual_rows(h), nt_dims, precision=HIGH, preferred_element_type=jnp.float32
+            )
+            for h in range(per)
+        ],
+        axis=0,
     )
     label_all().wait_recv()
     named = lbuf[0]
@@ -578,9 +617,12 @@
 
     k_all().wait_recv()
     columns = jnp.concatenate([kbuf[d] for d in range(ndev)], axis=0)
-    weight = jnp.dot(gram, columns, precision=HIGH, preferred_element_type=jnp.float32) - offset
+    both = jnp.dot(gram, columns, precision=HIGH, preferred_element_type=jnp.float32)
+    weight = -offset
+    for h in range(per):
+        weight = weight + both[h * own_s : (h + 1) * own_s, h * targets : (h + 1) * targets]
     weight = weight * (1.0 / (CHANNELS * 9.0**LAYERS))
-    wide = (weight[:, None, :] * keep[...][None]).reshape(own_s * groups, targets)
+    wide = (weight[:, None, :] * keep[:, :targets][None]).reshape(own_s * groups, targets)
     wexp[...] = jnp.dot(split_rows(wide), spread[...], preferred_element_type=jnp.float32)
     pred[...] = columns.T
 
@@ -598,9 +640,13 @@
             low = fold(sums[channel][0], sums[channel][1], even, SIDE)
             high = fold(sums[channel][2], sums[channel][3], even, SIDE)
             flat[channel, m] = fold(low, high, early, 2 * SIDE)
-    residual_ref[...] = jnp.dot(
-        pred[pl.ds(ti * own_t, own_t), :], duals, precision=HIGH, preferred_element_type=jnp.float32
-    ) - own_onehot[:own_t, :CLASSES]
+    residual = -own_onehot[:own_t, :CLASSES]
+    for h in range(per):
+        residual = residual + jnp.dot(
+            pred[pl.ds(h * targets + ti * own_t, own_t), :], dual_rows(h),
+            precision=HIGH, preferred_element_type=jnp.float32,
+        )
+    residual_ref[...] = residual
     for channel in range(CHANNELS):
         for s in range(SUB):
             grad_ref[channel, s] = flat[channel, :, s, :]
@@ -618,6 +664,7 @@
     groups = nt * groups_own
     chips = nt // 2
     ndev = nt * ns
+    per = sharing(nt * own_t, own_s)
     f32 = jnp.float32
     vmem = pl.BlockSpec(memory_space=pltpu.VMEM)
     hbm = pl.BlockSpec(memory_space=pltpu.HBM)
@@ -641,11 +688,11 @@
             pltpu.VMEM((nt, groups_own, CHANNELS * PACK) + tile, f32),
             pltpu.VMEM((ns,) + dual_weights.shape, f32),
             pltpu.VMEM((nt, 1, LANES), jnp.int32),
-            pltpu.VMEM((ndev, own_s, nt * own_t), f32),
+            pltpu.VMEM((ndev, own_s // per, per * nt * own_t), f32),
             pltpu.VMEM((2 * LANES, LANES), jnp.bfloat16),
-            pltpu.VMEM((3 * LANES, nt * own_t), jnp.bfloat16),
+            pltpu.VMEM((3 * LANES, per * nt * own_t), jnp.bfloat16),
             pltpu.VMEM((3 * nt * own_t, LANES), jnp.bfloat16),
-            pltpu.VMEM((groups, nt * own_t), f32),
+            pltpu.VMEM((groups, per * nt * own_t), f32),
             pltpu.VMEM((CHANNELS, PACK, own_s) + tile, f32),
             pltpu.VMEM((LAYERS, 2, PACK, own_s) + tile, f32),
             pltpu.VMEM((LAYERS, PACK, own_s) + tile, f32),
@@ -657,7 +704,7 @@
             pltpu.VMEM((groups, CHANNELS, PACK, own_s) + tile, f32),
             pltpu.VMEM((own_s, groups, LANES), f32),
             pltpu.VMEM((own_s * groups, LANES), f32),
-            pltpu.VMEM((nt * own_t, ns * dual_weights.shape[0]), f32),
+            pltpu.VMEM((per * nt * own_t, ns * dual_weights.shape[0] // per), f32),
             pltpu.VMEM((CHANNELS, own_s) + tile, f32),
             dma((4 + CHANNELS,)),
             dma,

time: 24.6 us -> 23.8 us (0.967)
  Pallas kernels: 23.7 us -> 23 us
    pallas_call x1, Pallas kernels: 23.1 us -> 22.4 us  [shards(): pl.pallas_call(functools.partial(kernel, nt, ns, own_t, own_s), out_shape...]
where the time goes in v4:
time: 23.8 us; the launch traced here: 23.7 us
  Pallas kernels  23 us (97%)
  between operations  0.64 us (3%)
    pallas_call x1, Pallas kernels, shards(): pl.pallas_call(functools.partial(kernel, nt, ns, own_t, own_s), out_shape...  22.4 us
    pallas_call x1, Pallas kernels, shards(): pl.pallas_call(hand_over, out_shape=(jax.ShapeDtypeStruct(residual.shape,...  0.63 us

profile of v4, /device:TPU:0, one launch (start us, length us, event | category | flops | bytes accessed | tf_op | source)
XLA Modules:
  0.0 23.7 jit_solution(123498770585891594)
XLA Ops:
  0.6 22.4 %shard_map.68 = (f32[8,100]{1,0:T(8,128)S(1)}, f32[3,8,4,128]{3,2,1,0:T(4,128)S(1)}) custom-call(s32[8]{0:T(128)} %index_hbm.1, s32[8]{0:T(128)} %label_hbm.1, f32[3,8,8,8,128]{4,3,2,1,0:T(8,128)} %bitcast.9, f32[32,100]{1,0:T(8,128)} %dual_hbm.1, f32[3,8,4,128]{3,2,1,0:T(4,128)} %bitcast.10), custom_call_target="tpu_custom_call" | custom-call | tf_op jit(solution)/shard_map/pallas_call | solution.py:675
  23.0 0.6 %shard_map.69 = (f32[8,100]{1,0:T(8,128)}, f32[3,8,4,128]{3,2,1,0:T(4,128)}) custom-call(f32[8,100]{1,0:T(8,128)S(1)} %get-tuple-element.6.residual_ref, f32[3,8,4,128]{3,2,1,0:T(4,128)S(1)} %get-tuple-element.7.grad_ref), custom_call_target="tpu_custom_call" | custom-call | tf_op jit(solution)/shard_map/pallas_call | solution.py:729

commit v5 on v4

--- a/solution.py
+++ b/solution.py
@@ -131,12 +131,15 @@
     return per if LANES % targets == 0 and own_s % per == 0 else 1
 
 
-def split_rows(v):
+def split_parts(v):
     high = v.astype(jnp.bfloat16)
     rest = v - high.astype(jnp.float32)
     middle = rest.astype(jnp.bfloat16)
-    low = (rest - middle.astype(jnp.float32)).astype(jnp.bfloat16)
-    return jnp.concatenate([high, middle, low], axis=1)
+    return high, middle, (rest - middle.astype(jnp.float32)).astype(jnp.bfloat16)
+
+
+def split_rows(v):
+    return jnp.concatenate(split_parts(v), axis=1)
 
 
 def fold(a, b, keep, shift):
@@ -149,7 +152,7 @@
     residual_ref, grad_ref,
     index_ref, label_ref, pool_a, pool_b, pool_c, support_ref,
     tbuf, dbuf, lbuf, kbuf, band, gathers, spread, keep, srep, sroot, shalf, tlev, mid, held, amp, ang, unit, ksum, wexp, pred, flat,
-    in_sem, plane_send, plane_recv, swap_send, part_send, part_recv,
+    in_sem, plane_send, plane_recv, swap_send, edge_send, part_send, part_recv,
     dual_send, dual_recv, label_send, label_recv, k_send, k_recv,
 ):
     ti = lax.axis_index("tgt")
@@ -172,12 +175,6 @@
     def greet(t, s):
         pl.semaphore_signal(barrier, inc=1, device_id=(t, s), device_id_type=MESH)
 
-    for step in range(1, ns):
-        greet(ti, lax.rem(si + step, ns))
-    greet(chip * 2 + 1 - core, si)
-    for step in range(1, chips):
-        greet(lax.rem(ti + 2 * step, nt), si)
-
     def fetch(at, src, dst):
         return pltpu.make_async_copy(src, dst, in_sem.at[at])
 
@@ -187,7 +184,16 @@
         fetch(2, dual_hbm, dbuf.at[si]),
         fetch(3, support_hbm, support_ref),
     ] + [fetch(4 + c, pool_hbm.at[c], pool_refs[c]) for c in range(CHANNELS)]
-    for at in (0, 4, 5, 6, 3, 2, 1):
+    for at in (0, 4, 5, 6):
+        loads[at].start()
+
+    for step in range(1, ns):
+        greet(ti, lax.rem(si + step, ns))
+    greet(chip * 2 + 1 - core, si)
+    for step in range(1, chips):
+        greet(lax.rem(ti + 2 * step, nt), si)
+
+    for at in (3, 2, 1):
         loads[at].start()
 
     def plane_copy(source_chip, gl, target_chip):
@@ -335,12 +341,30 @@
                         functools.partial(action, choice(h), target)
                     )
 
+    outward = (chip == 0) | (chip == chips - 2)
+    edge = outward | (chip == 1) | (chip == chips - 1)
+    mate = jnp.where(outward, chip + 1, chip - 1)
+    direct_pairs = share == 2 and chips > 3
+
+    def edge_copy(gl):
+        part = tbuf.at[ti, gl]
+        return pltpu.make_async_remote_copy(
+            src_ref=part,
+            dst_ref=part,
+            send_sem=edge_send,
+            recv_sem=plane_recv.at[chip, gl],
+            device_id=(mate * 2 + core, si),
+            device_id_type=MESH,
+        )
+
     each_plane(lambda gl, target: plane_copy(chip, gl, target).start())
     for h in range(0, groups_own, share):
         part_copy(chip, choice(h), core).start()
     if share == 2:
         for h in range(1, groups_own, share):
             take_group(choice(h))
+            if direct_pairs:
+                pl.when(edge)(functools.partial(lambda gl: edge_copy(gl).start(), choice(h)))
             part_copy(chip, choice(h), core).start()
 
     loads[2].wait()
@@ -446,7 +470,8 @@
         p = order(n)
         plane_copy(p, gl, chip).wait_recv()
         if share == 2:
-            pl.when(direct)(lambda: swap_copy(p, gl).start())
+            apart = ((p != mate) | jnp.logical_not(edge)) if direct_pairs else True
+            pl.when(direct & apart)(lambda: swap_copy(p, gl).start())
         part_copy(p, gl, core).start()
         return p * 2 + core, gl
 
@@ -588,6 +613,16 @@
         ],
         axis=0,
     )
+    top, middle, bottom = split_parts(gram)
+    blank = jnp.zeros_like(top)
+    factors = jnp.concatenate(
+        [
+            jnp.concatenate([top, top, top], axis=1),
+            jnp.concatenate([middle, middle, blank], axis=1),
+            jnp.concatenate([bottom, blank, blank], axis=1),
+        ],
+        axis=0,
+    )
     label_all().wait_recv()
     named = lbuf[0]
     for t in range(1, nt):
@@ -609,7 +644,13 @@
 
     sent(plane_send, chips - 1, groups_own // share)
     if share == 2:
-        sent(swap_send, chips - 1, groups_own // share)
+        half = groups_own // share
+        if direct_pairs:
+            pl.when(edge)(lambda: sent(swap_send, chips - 2, half))
+            pl.when(edge)(lambda: sent(edge_send, 1, half))
+            pl.when(jnp.logical_not(edge))(lambda: sent(swap_send, chips - 1, half))
+        else:
+            sent(swap_send, chips - 1, half)
     sent(part_send, chips, groups_own)
     dual_all().wait_send()
     label_all().wait_send()
@@ -617,7 +658,11 @@
 
     k_all().wait_recv()
     columns = jnp.concatenate([kbuf[d] for d in range(ndev)], axis=0)
-    both = jnp.dot(gram, columns, precision=HIGH, preferred_element_type=jnp.float32)
+    three = jnp.dot(
+        factors, jnp.concatenate(split_parts(columns), axis=0), preferred_element_type=jnp.float32
+    )
+    span = per * own_s
+    both = (three[2 * span :] + three[span : 2 * span]) + three[:span]
     weight = -offset
     for h in range(per):
         weight = weight + both[h * own_s : (h + 1) * own_s, h * targets : (h + 1) * targets]
@@ -711,6 +756,7 @@
             dma((chips, groups_own)),
             dma,
             dma,
+            dma,
             dma((chips, groups_own)),
             dma,
             dma,

time: 23.8 us -> 23.3 us (0.979)
  Pallas kernels: 23 us -> 22.5 us
    pallas_call x1, Pallas kernels: 22.4 us -> 21.9 us  [shards(): pl.pallas_call(functools.partial(kernel, nt, ns, own_t, own_s), out_shape...]
where the time goes in v5:
time: 23.3 us; the launch traced here: 23.2 us
  Pallas kernels  22.5 us (97%)
  between operations  0.64 us (3%)
    pallas_call x1, Pallas kernels, shards(): pl.pallas_call(functools.partial(kernel, nt, ns, own_t, own_s), out_shape...  21.9 us
    pallas_call x1, Pallas kernels, shards(): pl.pallas_call(hand_over, out_shape=(jax.ShapeDtypeStruct(residual.shape,...  0.63 us

profile of v5, /device:TPU:0, one launch (start us, length us, event | category | flops | bytes accessed | tf_op | source)
XLA Modules:
  0.0 23.2 jit_solution(8052117611607237096)
XLA Ops:
  0.6 21.9 %shard_map.68 = (f32[8,100]{1,0:T(8,128)S(1)}, f32[3,8,4,128]{3,2,1,0:T(4,128)S(1)}) custom-call(s32[8]{0:T(128)} %index_hbm.1, s32[8]{0:T(128)} %label_hbm.1, f32[3,8,8,8,128]{4,3,2,1,0:T(8,128)} %bitcast.9, f32[32,100]{1,0:T(8,128)} %dual_hbm.1, f32[3,8,4,128]{3,2,1,0:T(4,128)} %bitcast.10), custom_call_target="tpu_custom_call" | custom-call | tf_op jit(solution)/shard_map/pallas_call | solution.py:720
  22.5 0.6 %shard_map.69 = (f32[8,100]{1,0:T(8,128)}, f32[3,8,4,128]{3,2,1,0:T(4,128)}) custom-call(f32[8,100]{1,0:T(8,128)S(1)} %get-tuple-element.6.residual_ref, f32[3,8,4,128]{3,2,1,0:T(4,128)S(1)} %get-tuple-element.7.grad_ref), custom_call_target="tpu_custom_call" | custom-call | tf_op jit(solution)/shard_map/pallas_call | solution.py:775

commit v6 on v5

--- a/solution.py
+++ b/solution.py
@@ -579,7 +579,7 @@
             for k, v in enumerate(vertical(slope, mask)):
                 held[1, at, k] = v
 
-    span = 2
+    span = 4
     whole = max(groups - LAYERS, 0) // span
 
     def pair_unit(trip, carry):

time: 23.3 us -> 23.3 us (level)
  no operation moved by 1% of the time
where the time goes in v6:
time: 23.3 us; the launch traced here: 23.2 us
  Pallas kernels  22.5 us (97%)
  between operations  0.64 us (3%)
    pallas_call x1, Pallas kernels, shards(): pl.pallas_call(functools.partial(kernel, nt, ns, own_t, own_s), out_shape...  21.9 us
    pallas_call x1, Pallas kernels, shards(): pl.pallas_call(hand_over, out_shape=(jax.ShapeDtypeStruct(residual.shape,...  0.63 us

profile of v6, /device:TPU:0, one launch (start us, length us, event | category | flops | bytes accessed | tf_op | source)
XLA Modules:
  0.0 23.2 jit_solution(11580083271913572110)
XLA Ops:
  0.6 21.9 %shard_map.68 = (f32[8,100]{1,0:T(8,128)S(1)}, f32[3,8,4,128]{3,2,1,0:T(4,128)S(1)}) custom-call(s32[8]{0:T(128)} %index_hbm.1, s32[8]{0:T(128)} %label_hbm.1, f32[3,8,8,8,128]{4,3,2,1,0:T(8,128)} %bitcast.9, f32[32,100]{1,0:T(8,128)} %dual_hbm.1, f32[3,8,4,128]{3,2,1,0:T(4,128)} %bitcast.10), custom_call_target="tpu_custom_call" | custom-call | tf_op jit(solution)/shard_map/pallas_call | solution.py:720
  22.5 0.6 %shard_map.69 = (f32[8,100]{1,0:T(8,128)}, f32[3,8,4,128]{3,2,1,0:T(4,128)}) custom-call(f32[8,100]{1,0:T(8,128)S(1)} %get-tuple-element.6.residual_ref, f32[3,8,4,128]{3,2,1,0:T(4,128)S(1)} %get-tuple-element.7.grad_ref), custom_call_target="tpu_custom_call" | custom-call | tf_op jit(solution)/shard_map/pallas_call | solution.py:775
